TPU v7x, 32 devices: a whole 2x2x4 slice. The times are simulated.
32 devices in a mesh: dp: 8 (over z, y), mix: 4 (over x, core).
Axes of the slice: x: 2, y: 2, z: 4, core: 2. Of those that a mesh axis runs over, the one named last changes fastest.
Arguments:
- patches: bfloat16 [224, 196, 768], P('dp', 'mix'), may hold values from -6 to 6
- valid_counts: int32 [8], P('dp'), may hold values from 7 to 28, as said below
- gain_one: float32 [768], replicated, may hold values from 0.5 to 1.5
- shift_one: float32 [768], replicated, may hold values from -1.25 to 1.25
- tok_in: bfloat16 [196, 384], replicated, may hold values from -0.4375 to 0.4375
- tok_inbias: float32 [384], replicated, may hold values from -1.25 to 1.25
- tok_out: bfloat16 [384, 196], replicated, may hold values from -0.3125 to 0.3125
- tok_outbias: float32 [196], replicated, may hold values from -1.25 to 1.25
- gain_two: float32 [768], replicated, may hold values from 0.5 to 1.5
- shift_two: float32 [768], replicated, may hold values from -1.25 to 1.25
- chan_in: bfloat16 [768, 3072], replicated, may hold values from -0.21875 to 0.21875
- chan_inbias: float32 [3072], replicated, may hold values from -1.25 to 1.25
- chan_out: bfloat16 [3072, 768], replicated, may hold values from -0.109375 to 0.109375
- chan_outbias: float32 [768], replicated, may hold values from -1.25 to 1.25
- out_grad: bfloat16 [224, 196, 768], P('dp', 'mix'), may hold values from -6 to 6
Outputs:
- mixed_out: bfloat16 [224, 196, 768], P('dp', 'mix')
- patch_grad: bfloat16 [224, 196, 768], P('dp', 'mix')
- grad_gain_one: float32 [768], replicated
- grad_shift_one: float32 [768], replicated
- grad_tok_in: float32 [196, 384], replicated
- grad_tok_inbias: float32 [384], replicated
- grad_tok_out: float32 [384, 196], replicated
- grad_tok_outbias: float32 [196], replicated
- grad_gain_two: float32 [768], replicated
- grad_shift_two: float32 [768], replicated
- grad_chan_in: float32 [768, 3072], replicated
- grad_chan_inbias: float32 [3072], replicated
- grad_chan_out: float32 [3072, 768], replicated
- grad_chan_outbias: float32 [768], replicated
Inputs may be any that keep to these rules, and one draw needn't show every extreme that they name: `valid_counts`: how many of the 28 images of each index of dp are real; the rest are padding and get no gradient.
All inputs are finite; a program needn't handle non-finite values.
Results may differ from a plain program's by a relative error of at most 0.008.
Values may be sent and summed in bfloat16 or wider, within the bound.
A program may use at most 192 MiB of HBM per device.

v0:
```python
import jax
import jax.numpy as jnp
from jax import lax
from jax.sharding import PartitionSpec as P

EPS = 1e-06


def layer_norm(values, gain, shift):
    center = values - jnp.mean(values, axis=-1, keepdims=True)
    spread = jnp.mean(center * center, axis=-1, keepdims=True)
    return center * lax.rsqrt(spread + EPS) * gain + shift


def shards(
    patches,
    valid_counts,
    gain_one,
    shift_one,
    tok_in,
    tok_inbias,
    tok_out,
    tok_outbias,
    gain_two,
    shift_two,
    chan_in,
    chan_inbias,
    chan_out,
    chan_outbias,
    out_grad,
):
    images, part, width = patches.shape
    rowcount = images * part
    inputs = patches.astype(jnp.float32)
    normed_full, first_back = jax.vjp(layer_norm, inputs, gain_one, shift_one)
    normed = normed_full.astype(jnp.bfloat16)
    columns = lax.all_to_all(normed, "mix", split_axis=2, concat_axis=1, tiled=True)
    widened = (
        jnp.einsum("bsc,sk->bkc", columns, tok_in, preferred_element_type=jnp.float32)
        + tok_inbias[None, :, None]
    )
    hidden = jax.nn.gelu(widened).astype(jnp.bfloat16)
    mixed_cols = (
        jnp.einsum("bkc,ks->bsc", hidden, tok_out, preferred_element_type=jnp.float32)
        + tok_outbias[None, :, None]
    ).astype(jnp.bfloat16)
    mixed = lax.all_to_all(mixed_cols, "mix", split_axis=1, concat_axis=2, tiled=True)
    middle = inputs + mixed.astype(jnp.float32)
    second_full, second_back = jax.vjp(layer_norm, middle, gain_two, shift_two)
    second = second_full.astype(jnp.bfloat16).reshape(rowcount, width)
    inner = jnp.dot(second, chan_in, preferred_element_type=jnp.float32) + chan_inbias
    activ = jax.nn.gelu(inner).astype(jnp.bfloat16)
    branch = jnp.dot(activ, chan_out, preferred_element_type=jnp.float32) + chan_outbias
    mixed_out = (middle + branch.reshape(images, part, width)).astype(jnp.bfloat16)
    live = jnp.arange(images, dtype=jnp.int32) < valid_counts[0]
    upstream = jnp.where(live[:, None, None], out_grad, jnp.zeros_like(out_grad)).reshape(
        rowcount, width
    )
    inner_again = jnp.dot(second, chan_in, preferred_element_type=jnp.float32) + chan_inbias
    activ_full, chan_gelu_back = jax.vjp(jax.nn.gelu, inner_again)
    activ_again = activ_full.astype(jnp.bfloat16)
    grad_chan_out = jnp.einsum(
        "rf,rc->fc", activ_again, upstream, preferred_element_type=jnp.float32
    )
    grad_chan_outbias = jnp.sum(upstream.astype(jnp.float32), axis=0)
    grad_activ = jnp.einsum("rc,fc->rf", upstream, chan_out, preferred_element_type=jnp.float32)
    grad_inner = chan_gelu_back(grad_activ)[0].astype(jnp.bfloat16)
    grad_chan_in = jnp.einsum("rc,rf->cf", second, grad_inner, preferred_element_type=jnp.float32)
    grad_chan_inbias = jnp.sum(grad_inner.astype(jnp.float32), axis=0)
    grad_second = jnp.einsum("rf,cf->rc", grad_inner, chan_in, preferred_element_type=jnp.float32)
    grad_middle, grad_gain_two, grad_shift_two = second_back(
        grad_second.reshape(images, part, width)
    )
    grad_middle = grad_middle + upstream.astype(jnp.float32).reshape(images, part, width)
    grad_cols = lax.all_to_all(
        grad_middle.astype(jnp.bfloat16), "mix", split_axis=2, concat_axis=1, tiled=True
    )
    widened_again = (
        jnp.einsum("bsc,sk->bkc", columns, tok_in, preferred_element_type=jnp.float32)
        + tok_inbias[None, :, None]
    )
    hidden_full, tok_gelu_back = jax.vjp(jax.nn.gelu, widened_again)
    hidden_again = hidden_full.astype(jnp.bfloat16)
    grad_tok_out = jnp.einsum(
        "bkc,bsc->ks", hidden_again, grad_cols, preferred_element_type=jnp.float32
    )
    grad_tok_outbias = jnp.sum(grad_cols.astype(jnp.float32), axis=(0, 2))
    grad_hidden = jnp.einsum("ks,bsc->bkc", tok_out, grad_cols, preferred_element_type=jnp.float32)
    grad_widened = tok_gelu_back(grad_hidden)[0].astype(jnp.bfloat16)
    grad_tok_in = jnp.einsum(
        "bsc,bkc->sk", columns, grad_widened, preferred_element_type=jnp.float32
    )
    grad_tok_inbias = jnp.sum(grad_widened.astype(jnp.float32), axis=(0, 2))
    grad_columns = jnp.einsum(
        "sk,bkc->bsc", tok_in, grad_widened, preferred_element_type=jnp.float32
    ).astype(jnp.bfloat16)
    grad_normed = lax.all_to_all(grad_columns, "mix", split_axis=1, concat_axis=2, tiled=True)
    grad_inputs, grad_gain_one, grad_shift_one = first_back(grad_normed.astype(jnp.float32))
    patch_grad = (grad_middle + grad_inputs).astype(jnp.bfloat16)
    summed = lax.psum(
        (
            grad_gain_one,
            grad_shift_one,
            grad_tok_in,
            grad_tok_inbias,
            grad_tok_out,
            grad_tok_outbias,
            grad_gain_two,
            grad_shift_two,
            grad_chan_in,
            grad_chan_inbias,
            grad_chan_out,
            grad_chan_outbias,
        ),
        ("dp", "mix"),
    )
    return (
        mixed_out,
        patch_grad,
        summed[0],
        summed[1],
        summed[2],
        summed[3],
        summed[4],
        summed[5],
        summed[6],
        summed[7],
        summed[8],
        summed[9],
        summed[10],
        summed[11],
    )


def solution(mesh):
    return jax.shard_map(
        shards,
        mesh=mesh,
        in_specs=(
            P("dp", "mix", None),
            P("dp"),
            P(),
            P(),
            P(),
            P(),
            P(),
            P(),
            P(),
            P(),
            P(),
            P(),
            P(),
            P(),
            P("dp", "mix", None),
        ),
        out_specs=(
            P("dp", "mix", None),
            P("dp", "mix", None),
            P(),
            P(),
            P(),
            P(),
            P(),
            P(),
            P(),
            P(),
            P(),
            P(),
            P(),
            P(),
        ),
        check_vma=False,
    )
```

profile of v0, /device:TPU:0, one launch (start us, length us, event | category | flops | bytes accessed | tf_op | source)
XLA Modules:
  0.0 723.8 jit_solution(6114710992727440725)
XLA Ops:
  15.3 11.4 %copy.67 = bf16[28,49,768]{1,0,2:T(8,128)(2,1)} copy(bf16[28,49,768]{2,1,0:T(8,128)(2,1)} %fusion.25) | data formatting | bytes 4214784 | tf_op jit(solution)/shard_map/convert_element_type | solution.py:36
  26.7 11.5 %reshape.138 = bf16[4,2,131712]{2,1,0:T(2,128)(2,1)} reshape(bf16[768,28,49]{2,1,0:T(8,128)(2,1)} %bitcast.86) | data formatting | bytes 4214784
  38.2 31.0 %all_to_all.54 = bf16[4,2,131712]{2,1,0:T(2,128)(2,1)} all-to-all(bf16[4,2,131712]{2,1,0:T(2,128)(2,1)} %reshape.138), channel_id=1, replica_groups=mesh['dp'=8,'mix'=4] {'mix'}, dimensions={0} | all-to-all | bytes 4214784 | tf_op jit(solution)/shard_map/all_to_all | solution.py:37
  69.3 11.9 %reshape.139 = bf16[768,28,49]{2,1,0:T(8,128)(2,1)} reshape(bf16[4,2,131712]{2,1,0:T(2,128)(2,1)} %all_to_all.54) | data formatting | bytes 4214784
  81.2 9.6 %copy.68 = bf16[28,49,4,192]{3,1,2,0:T(8,128)(2,1)} copy(bf16[28,49,4,192]{1,0,3,2:T(8,128)(2,1)} %bitcast.84) | data formatting | bytes 4214784 | tf_op jit(solution)/shard_map/all_to_all | solution.py:37
  90.8 5.7 all_to_all.43
  96.5 7.8 %fusion.17 = (bf16[28,384,192]{1,2,0:T(8,128)(2,1)S(1)}, f32[28,192,384]{2,1,0:T(8,128)}) fusion(f32[384]{0:T(512)S(1)} %copy-done.29, bf16[28,196,192]{2,1,0:T(8,128)(2,1)} %all_to_all.43, bf16[196,384]{1,0:T(8,128)(2,1)S(1)} %copy-done), kind=kOutput, calls=%fused_computation.26 | convolution fusion | flops 829882368 | bytes 14645760 | tf_op jit(solution)/shard_map/bsc,sk->bkc/dot_general | solution.py:39
  109.5 7.4 %copy.70 = bf16[28,196,192]{2,0,1:T(8,128)(2,1)} copy(bf16[28,196,192]{1,2,0:T(8,128)(2,1)} %fusion.30) | data formatting | bytes 4214784 | tf_op jit(solution)/shard_map/convert_element_type | solution.py:46
  116.8 4.9 all-to-all-start.1
  122.4 4.5 convert_reduce_fusion.4
  126.9 4.0 reshape.128
  130.9 28.5 %all-to-all-done.1 = bf16[28,196,192]{2,0,1:T(8,128)(2,1)} async-done(((bf16[28,196,192]{2,0,1:T(8,128)(2,1)}), bf16[28,196,192]{2,0,1:T(8,128)(2,1)}, u32[]{:S(2)}, u32[]{:S(2)}) %all-to-all-start.1) | async-done | bytes 2107424 | tf_op jit(solution)/shard_map/all_to_all | solution.py:47
  159.4 7.5 %copy.71 = bf16[28,196,192]{1,2,0:T(8,128)(2,1)} copy(bf16[28,196,192]{2,0,1:T(8,128)(2,1)} %all-to-all-done.1) | data formatting | bytes 4214784 | tf_op jit(solution)/shard_map/all_to_all | solution.py:47
  166.8 5.2 copy.72
  172.0 6.9 reshape.132
  178.9 7.5 %copy.73 = f32[28,49,4,192]{3,2,1,0:T(4,128)} copy(f32[28,49,4,192]{3,1,2,0:T(8,128)} %bitcast.82) | data formatting | bytes 8429568 | tf_op jit(solution)/shard_map/convert_element_type | solution.py:48
  186.4 7.7 %reshape.130 = f32[28,49,768]{2,1,0:T(8,128)} reshape(f32[28,49,4,192]{3,2,1,0:T(4,128)} %copy.73) | data formatting | bytes 8429568 | tf_op jit(solution)/shard_map/convert_element_type | solution.py:48
  202.2 18.0 %multiply_convert_fusion = (bf16[1372,3072]{1,0:T(8,128)(2,1)}, f32[1372,3072]{1,0:T(8,128)}) fusion(f32[3072]{0:T(1024)S(1)} %copy-done.27, bf16[1372,768]{1,0:T(8,128)(2,1)} %reshape.126, bf16[768,3072]{1,0:T(8,128)(2,1)} %param.25), kind=kOutput, calls=%fused_computation.10 | convolution fusion | flops 6516056064 | bytes 32126976 | tf_op jit(solution)/shard_map/dot_general | solution.py:51
  220.2 19.9 %convert_reduce_fusion = (f32[3072]{0:T(1024)S(1)}, bf16[1372,3072]{1,0:T(8,128)(2,1)S(1)}) fusion(f32[1372,3072]{1,0:T(8,128)} %get-tuple-element.40, f32[3072]{0:T(1024)S(1)} %copy-done.27, bf16[1372,768]{1,0:T(8,128)(2,1)S(1)} %copy-done.11, bf16[3072,768]{1,0:T(8,128)(2,1)} %param.27), kind=kOutput, calls=%fused_computation.9 | convolution fusion | flops 6570845184 | bytes 32139264 | tf_op jit(solution)/shard_map/rc,fc->rf/dot_general | solution.py:66
  240.1 8.3 %fusion.41 = (f32[768]{0:T(1024)S(1)}, f32[1372,768]{1,0:T(8,128)}) fusion(bf16[1372,3072]{1,0:T(8,128)(2,1)S(1)} %get-tuple-element.46, bf16[768,3072]{1,0:T(8,128)(2,1)S(1)} %bitcast.92), kind=kOutput, calls=%fused_computation.81 | convolution fusion | flops 6474960896 | bytes 17366016 | tf_op jit(solution)/shard_map/rf,cf->rc/dot_general | solution.py:70
  248.5 5.1 reshape.129
  253.6 4.7 multiply_reduce_fusion
  258.3 12.0 %convolution_add_fusion = f32[1372,768]{1,0:T(8,128)} fusion(bf16[1372,3072]{1,0:T(8,128)(2,1)} %get-tuple-element.39, bf16[3072,768]{1,0:T(8,128)(2,1)} %param.27, f32[768]{0:T(1024)S(1)} %copy-done.28), kind=kOutput, calls=%fused_computation.54 | convolution fusion | flops 6474961920 | bytes 17366016 | tf_op jit(solution)/shard_map/dot_general | solution.py:53
  270.3 5.2 reshape.127
  275.5 7.4 %fusion.39 = (f32[28,49]{1,0:T(8,128)S(1)}, f32[28,49,768]{2,1,0:T(8,128)S(1)}, bf16[28,49,768]{2,1,0:T(8,128)(2,1)}) fusion(f32[28,49]{1,0:T(8,128)S(1)} %multiply_multiply_fusion.5, f32[28,49,768]{2,1,0:T(8,128)} %copy-done.1, f32[28,49]{1,0:T(8,128)S(1)} %broadcast_multiply_fusion, f32[28,49]{1,0:T(8,128)S(1)} %fusion.38, f32[28,49,768]{2,1,0:T(8,128)} %reshape.129, ...), kind=kLoop, calls=%fused_computation.79 | loop fusion | flops 9481892 | bytes 18991552 | tf_op jit(solution)/shard_map/transpose(jvp())/reduce_sum | solution.py:10
  285.7 10.8 %copy.74 = bf16[28,49,768]{1,0,2:T(8,128)(2,1)} copy(bf16[28,49,768]{2,1,0:T(8,128)(2,1)S(1)} %fusion.29) | data formatting | bytes 4214784 | tf_op jit(solution)/shard_map/convert_element_type | solution.py:76
  296.5 11.5 %reshape.140 = bf16[4,2,131712]{2,1,0:T(2,128)(2,1)} reshape(bf16[768,28,49]{2,1,0:T(8,128)(2,1)} %bitcast.87) | data formatting | bytes 4214784
  311.7 13.5 %fusion.43 = f32[3072,768]{1,0:T(8,128)} fusion(bf16[1372,3072]{1,0:T(8,128)(2,1)} %get-tuple-element.39, bf16[1372,768]{1,0:T(8,128)(2,1)} %reshape.128), kind=kOutput, calls=%fused_computation.83 | convolution fusion | flops 6473908224 | bytes 19974144 | tf_op jit(solution)/shard_map/rf,rc->fc/dot_general | solution.py:62
  325.2 12.2 %fusion.42 = f32[768,3072]{1,0:T(8,128)} fusion(bf16[1372,768]{1,0:T(8,128)(2,1)S(1)} %copy-done.12, bf16[1372,3072]{1,0:T(8,128)(2,1)} %copy-done.33), kind=kOutput, calls=%fused_computation.82 | convolution fusion | flops 6473908224 | bytes 19974144 | tf_op jit(solution)/shard_map/rc,rf->cf/dot_general | solution.py:68
  337.4 10.9 %reshape.141 = bf16[768,28,49]{2,1,0:T(8,128)(2,1)} reshape(bf16[4,2,131712]{2,1,0:T(2,128)(2,1)S(1)} %all-to-all-done.2) | data formatting | bytes 4214784
  348.4 8.6 %copy.75 = bf16[28,49,4,192]{3,1,2,0:T(8,128)(2,1)S(1)} copy(bf16[28,49,4,192]{1,0,3,2:T(8,128)(2,1)} %bitcast.85) | data formatting | bytes 4214784 | tf_op jit(solution)/shard_map/all_to_all | solution.py:75
  359.9 5.2 convolution_bitcast_fusion
  365.1 9.6 %convert_reduce_fusion.1 = (f32[384]{0:T(512)S(1)}, bf16[28,384,192]{1,2,0:T(8,128)(2,1)S(1)}) fusion(f32[28,192,384]{2,1,0:T(8,128)} %get-tuple-element.38, f32[384]{0:T(512)S(1)} %copy-done.30, bf16[28,196,192]{2,1,0:T(8,128)(2,1)S(1)} %copy-done.10, bf16[384,196]{0,1:T(8,128)(2,1)S(1)} %copy-done.26), kind=kOutput, calls=%fused_computation.27 | convolution fusion | flops 856718976 | bytes 14647296 | tf_op jit(solution)/shard_map/ks,bsc->bkc/dot_general | solution.py:88
  378.9 5.4 convert_bitcast_fusion
  384.3 7.5 %copy.77 = bf16[28,196,192]{2,0,1:T(8,128)(2,1)} copy(bf16[28,196,192]{1,2,0:T(8,128)(2,1)} %convert_bitcast_fusion) | data formatting | bytes 4214784 | tf_op jit(solution)/shard_map/convert_element_type | solution.py:96
  391.8 4.7 all-to-all-start.3
  397.2 55.7 %all-to-all-done.3 = bf16[28,196,192]{2,0,1:T(8,128)(2,1)} async-done(((bf16[28,196,192]{2,0,1:T(8,128)(2,1)}), bf16[28,196,192]{2,0,1:T(8,128)(2,1)}, u32[]{:S(2)}, u32[]{:S(2)}) %all-to-all-start.3) | async-done | bytes 2107424 | tf_op jit(solution)/shard_map/all_to_all | solution.py:97
  453.0 7.0 copy.78
  459.9 3.8 copy.79
  463.8 7.0 reshape.133
  470.8 7.5 %copy.80 = f32[28,49,4,192]{3,2,1,0:T(4,128)} copy(f32[28,49,4,192]{3,1,2,0:T(8,128)} %bitcast.83) | data formatting | bytes 8429568 | tf_op jit(solution)/shard_map/convert_element_type | solution.py:98
  478.3 8.0 %reshape.131 = f32[28,49,768]{2,1,0:T(8,128)} reshape(f32[28,49,4,192]{3,2,1,0:T(4,128)} %copy.80) | data formatting | bytes 8429568 | tf_op jit(solution)/shard_map/convert_element_type | solution.py:98
  488.8 3.7 fusion.28
  496.3 42.5 %all-reduce = (f32[768]{0:T(1024)}, f32[768]{0:T(1024)}, f32[384]{0:T(512)}, f32[196]{0:T(256)}, f32[768]{0:T(1024)}, /*index=5*/f32[768]{0:T(1024)}, f32[3072]{0:T(1024)}, f32[768]{0:T(1024)}) all-reduce(f32[768]{0:T(1024)S(1)} %get-tuple-element.16, f32[768]{0:T(1024)S(1)} %reduce_sum.199, ...), channel_id=1, replica_groups=mesh['dp'=8,'mix'=4] {'dp','mix'}, use_global_device_ids=true, to_apply=%region_9.10 | all-reduce | flops 7492 | bytes 59936 | tf_op jit(solution)/shard_map/psum | solution.py:100
  538.8 6.7 add_convert_fusion.1
  545.5 155.2 %all-reduce.4.cloned.1.call-done = (f32[196,384]{1,0:T(8,128)}, f32[384,196]{0,1:T(8,128)}, f32[768,3072]{1,0:T(8,128)}, f32[3072,768]{1,0:T(8,128)}) async-done(((f32[196,384]{1,0:T(8,128)}, f32[384,196]{0,1:T(8,128)}, f32[768,3072]{1,0:T(8,128)}, f32[3072,768]{1,0:T(8,128)}), (f32[196,384]{1,0:T(8,128)}, f32[384,196]{0,1:T(8,128)}, f32[768,3072]{1,0:T(8,128)}, ...) | async-done | bytes 19476496 | tf_op jit(solution)/shard_map/psum | solution.py:100
  704.3 8.8 %copy.95 = f32[768,3072]{1,0:T(8,128)} copy(f32[768,3072]{1,0:T(8,128)} %get-tuple-element.57) | data formatting | bytes 18874368
  713.0 3.7 copy.96
  (114 shorter events, 45.3 us)
Async XLA Ops:
  7.2 89.3 %copy-start = (bf16[196,384]{1,0:T(8,128)(2,1)S(1)}, bf16[196,384]{1,0:T(8,128)(2,1)}, u32[]{:S(2)}) copy-start(bf16[196,384]{1,0:T(8,128)(2,1)} %param.19) | copy-start | bytes 451588
  7.2 6.0 copy-start.2
  7.2 6.0 copy-start.19
  7.2 6.0 copy-start.23
  9.5 3.1 copy-start.13
  12.0 0.6 copy-start.17
  12.6 0.6 copy-start.15
  90.8 5.7 copy-start.29
  96.5 9.8 %copy-start.25 = (bf16[384,196]{0,1:T(8,128)(2,1)S(1)}, bf16[384,196]{0,1:T(8,128)(2,1)}, u32[]{:S(2)}) copy-start(bf16[384,196]{0,1:T(8,128)(2,1)} %param.21) | copy-start | bytes 451588
  96.5 9.8 %copy-start.31 = (f32[196]{0:T(256)S(1)}, f32[196]{0:T(256)}, u32[]{:S(2)}) copy-start(f32[196]{0:T(256)} %param.22) | copy-start | bytes 2356
  104.4 1.9 copy-start.32
  116.8 42.6 %all-to-all-start.1 = ((bf16[28,196,192]{2,0,1:T(8,128)(2,1)}), bf16[28,196,192]{2,0,1:T(8,128)(2,1)}, u32[]{:S(2)}, u32[]{:S(2)}) async-start(bf16[28,196,192]{2,0,1:T(8,128)(2,1)} %copy.70), calls=%async_computation.1 | async-start | bytes 6422528 | tf_op jit(solution)/shard_map/all_to_all | solution.py:47
  197.1 2.2 copy-start.1
  197.1 2.1 copy-start.21
  197.1 2.1 copy-start.24
  199.2 2.9 copy-start.27
  202.2 18.0 %copy-start.11 = (bf16[1372,768]{1,0:T(8,128)(2,1)S(1)}, bf16[1372,768]{1,0:T(8,128)(2,1)}, u32[]{:S(2)}) copy-start(bf16[1372,768]{1,0:T(8,128)(2,1)} %reshape.128) | copy-start | bytes 6322180
  202.2 37.9 %slice-start.3 = ((s8[4718592]{0:T(1024)(128)(4,1)}), s8[4194304]{0:T(1024)(128)(4,1)S(1)}, s32[]{:S(2)}) async-start(s8[4718592]{0:T(1024)(128)(4,1)} %bitcast.91), calls=%async_computation.8 | async-start | bytes 8388608
  220.2 20.0 %slice-start.4 = ((s8[4718592]{0:T(1024)(128)(4,1)}), s8[524288]{0:T(1024)(128)(4,1)S(1)}, s32[]{:S(2)}) async-start(s8[4718592]{0:T(1024)(128)(4,1)} %bitcast.91), calls=%async_computation.9 | async-start | bytes 1048576
  240.1 8.4 %copy-start.33 = (bf16[1372,3072]{1,0:T(8,128)(2,1)}, bf16[1372,3072]{1,0:T(8,128)(2,1)S(1)}, u32[]{:S(2)}) copy-start(bf16[1372,3072]{1,0:T(8,128)(2,1)S(1)} %get-tuple-element.46) | copy-start | bytes 25288708
  253.6 4.7 copy-start.28
  275.5 9.6 %copy-start.6 = (bf16[28,49,768]{2,1,0:T(8,128)(2,1)S(1)}, bf16[28,49,768]{2,1,0:T(8,128)(2,1)}, u32[]{:S(2)}) copy-start(bf16[28,49,768]{2,1,0:T(8,128)(2,1)} %get-tuple-element.31) | copy-start | bytes 6322180
  282.9 2.2 copy-start.5
  308.0 29.4 %all-to-all-start.2 = ((bf16[4,2,131712]{2,1,0:T(2,128)(2,1)}), bf16[4,2,131712]{2,1,0:T(2,128)(2,1)S(1)}, u32[]{:S(2)}, u32[]{:S(2)}) async-start(bf16[4,2,131712]{2,1,0:T(2,128)(2,1)} %reshape.140), calls=%async_computation.2 | async-start | bytes 4214784 | tf_op jit(solution)/shard_map/all_to_all | solution.py:75
  311.7 389.0 %all-reduce.4.cloned.1.call-start = ((), (), s32[]{:S(2)}) async-start(), calls=%async_computation.4 | async-start | bytes 38977536 | tf_op jit(solution)/shard_map/psum | solution.py:100
  311.7 13.5 %copy-start.12 = (bf16[1372,768]{1,0:T(8,128)(2,1)S(1)}, bf16[1372,768]{1,0:T(8,128)(2,1)}, u32[]{:S(2)}) copy-start(bf16[1372,768]{1,0:T(8,128)(2,1)} %reshape.126) | copy-start | bytes 6322180
  359.9 5.2 copy-start.10
  359.9 5.2 copy-start.26
  359.9 5.2 copy-start.30
  365.1 11.6 %copy-start.9 = (bf16[28,196,192]{2,1,0:T(8,128)(2,1)S(1)}, bf16[28,196,192]{2,1,0:T(8,128)(2,1)}, u32[]{:S(2)}) copy-start(bf16[28,196,192]{2,1,0:T(8,128)(2,1)} %all_to_all.43) | copy-start | bytes 6322180
  374.7 2.0 copy-start.8
  391.8 61.1 %all-to-all-start.3 = ((bf16[28,196,192]{2,0,1:T(8,128)(2,1)}), bf16[28,196,192]{2,0,1:T(8,128)(2,1)}, u32[]{:S(2)}, u32[]{:S(2)}) async-start(bf16[28,196,192]{2,0,1:T(8,128)(2,1)} %copy.77), calls=%async_computation.3 | async-start | bytes 6422528 | tf_op jit(solution)/shard_map/all_to_all | solution.py:97
  459.9 10.8 %copy-start.7 = (bf16[28,196,192]{1,2,0:T(8,128)(2,1)}, bf16[28,196,192]{1,2,0:T(8,128)(2,1)S(1)}, u32[]{:S(2)}) copy-start(bf16[28,196,192]{1,2,0:T(8,128)(2,1)S(1)} %copy.78) | copy-start | bytes 6322180
  478.3 10.5 %copy-start.3 = (bf16[28,49,768]{2,1,0:T(8,128)(2,1)S(1)}, bf16[28,49,768]{2,1,0:T(8,128)(2,1)}, u32[]{:S(2)}) copy-start(bf16[28,49,768]{2,1,0:T(8,128)(2,1)} %param.15) | copy-start | bytes 6322180
  478.3 10.5 %copy-start.14 = (f32[28,49]{1,0:T(8,128)S(1)}, f32[28,49]{1,0:T(8,128)}, u32[]{:S(2)}) copy-start(f32[28,49]{1,0:T(8,128)} %copy-done.13) | copy-start | bytes 16468
  478.3 10.5 %copy-start.20 = (f32[768]{0:T(1024)S(1)}, f32[768]{0:T(1024)}, u32[]{:S(2)}) copy-start(f32[768]{0:T(1024)} %param.17) | copy-start | bytes 9220
  488.5 4.0 copy-start.18
  488.5 4.1 copy-start.16
  488.8 4.9 copy-start.4
  492.6 3.7 copy-start.22
  702.4 10.6 %slice-start = ((s8[9437184]{0:T(1024)(128)(4,1)}), s8[4194304]{0:T(1024)(128)(4,1)S(1)}, s32[]{:S(2)}) async-start(s8[9437184]{0:T(1024)(128)(4,1)} %bitcast.89), calls=%async_computation.5 | async-start | bytes 8388608
  704.3 8.8 %slice-start.1 = ((s8[9437184]{0:T(1024)(128)(4,1)}), s8[4194304]{0:T(1024)(128)(4,1)S(1)}, s32[]{:S(2)}) async-start(s8[9437184]{0:T(1024)(128)(4,1)} %bitcast.89), calls=%async_computation.6 | async-start | bytes 8388608
  704.3 8.8 %slice-start.2 = ((s8[9437184]{0:T(1024)(128)(4,1)}), s8[1048576]{0:T(1024)(128)(4,1)S(1)}, s32[]{:S(2)}) async-start(s8[9437184]{0:T(1024)(128)(4,1)} %bitcast.89), calls=%async_computation.7 | async-start | bytes 2097152
Sparse Core Ops, SparseCore 0:
  379.0 321.6 all-reduce.3
where the time goes:
time: 731 us; the launch traced here: 724 us
  waiting for transfers between devices  239 us (33%)
  local copies, waits for them, and re-layouts  220 us (30%)
  matrix products  117 us (16%)
  blocking collectives  73.5 us (10%)
  other arithmetic  44.7 us (6%)
  between operations  15.3 us (2%)
  starting transfers between devices  13.2 us (2%)
    psum x1, waiting for transfers between devices, shards(): lax.psum((grad_gain_one, grad_shift_one, grad_tok_in, grad_tok_inbias, gr...  155 us
    unnamed x86, local copies, waits for them, and re-layouts  71.9 us
    all_to_all x1, waiting for transfers between devices, shards(): lax.all_to_all(grad_columns, 'mix', split_axis=1, concat_axis=2, tiled=True)  55.7 us
    psum x1, blocking collectives, shards(): lax.psum((grad_gain_one, grad_shift_one, grad_tok_in, grad_tok_inbias, gr...  42.5 us
    all_to_all x1, blocking collectives, shards(): lax.all_to_all(normed, 'mix', split_axis=2, concat_axis=1, tiled=True)  31 us
    all_to_all x1, waiting for transfers between devices, shards(): lax.all_to_all(mixed_cols, 'mix', split_axis=1, concat_axis=2, tiled=True)  28.5 us
    convert_element_type x4, local copies, waits for them, and re-layouts, shards(): middle = inputs + mixed.astype(jnp.float32)  27.2 us
    convert_element_type x4, local copies, waits for them, and re-layouts, shards(): grad_normed.astype(jnp.float32)  26.3 us
  transfers between devices with their start and end apart: 4, of which 3 were waited for; matrix products, arithmetic and copies ran while one was open for 13% of the time, Pallas kernels for 0%

commit v1 on v0

v1 whole, which is shorter than its diff:
```python
import functools

import jax
import jax.numpy as jnp
from jax import lax
from jax.experimental import pallas as pl
from jax.experimental.pallas import tpu as pltpu
from jax.sharding import PartitionSpec as P

EPS = 1e-06
SQ = 0.7978845608028654
CU = 0.044715
GROUP = 8
SLAB = 64
FC = 256
NT = (((1,), (1,)), ((), ()))
F32 = jnp.float32
BF16 = jnp.bfloat16
MESH = pl.DeviceIdType.MESH


def gelu_and_slope(v):
    v2 = v * v
    t = jnp.tanh(v * (SQ + (SQ * CU) * v2))
    h = 0.5 * v
    return h + h * t, 0.5 + 0.5 * t + h * (1.0 - t * t) * (SQ + (3.0 * SQ * CU) * v2)


def gelu(v):
    h = 0.5 * v
    return h + h * jnp.tanh(v * (SQ + (SQ * CU) * (v * v)))


def normalise(v):
    c = v - jnp.mean(v, axis=-1, keepdims=True)
    r = lax.rsqrt(jnp.mean(c * c, axis=-1, keepdims=True) + EPS)
    return c * r, r


def dot(a, b):
    return jnp.dot(a, b, preferred_element_type=F32)


def dot_nt(a, b):
    return lax.dot_general(a, b, NT, preferred_element_type=F32)


def flip(index, bit, step):
    return index + step - 2 * step * bit


def layer_kernel(
    dims,
    patches,
    out_grad,
    valid,
    tok_in,
    tok_out_t,
    chan_in,
    chan_out,
    gain_one,
    shift_one,
    gain_two,
    shift_two,
    tok_inbias,
    tok_outbias,
    chan_inbias,
    chan_outbias,
    mixed_out,
    patch_grad,
    sums,
    w1,
    w2,
    xin,
    uin,
    mo,
    rows32,
    tin,
    tin_t,
    tout,
    tout_t,
    mixed_keep,
    sec,
    sec_t,
    ups,
    ups_t,
    gsec,
    gi_s,
    act_s,
    d_tin,
    d_tout,
    vecs,
    d_b1,
    d_tb,
    blk,
    r0,
    r1,
    r2,
    r3,
    r4,
    wsem,
    osem,
    xs_s,
    xs_r,
    us_s,
    us_r,
    ms_s,
    ms_r,
    ps_s,
    ps_r,
    as_s,
    as_r,
    free,
):
    ni, part, width, ds, dc = dims
    nc = dc // FC
    rows = 4 * SLAB
    last = nc + ni
    me = lax.axis_index("mix")
    dp = lax.axis_index("dp")
    core = lax.rem(me, 2)
    xb = me // 2
    yb = lax.rem(dp, 2)
    zab = lax.rem(dp // 2, 2)
    zbb = lax.rem(dp // 4, 2)
    sib = flip(me, core, 1)
    xp = flip(me, xb, 2)
    diag = 3 - me
    peers = (xp, diag, sib)
    dev_sib = (dp, sib)
    dev_x = (dp, xp)
    dev_y = (flip(dp, yb, 1), me)
    dev_za = (flip(dp, zab, 2), me)
    dev_zb = (flip(dp, zbb, 4), me)

    wcopy1 = pltpu.make_async_copy(chan_in, w1, wsem.at[0])
    wcopy2 = pltpu.make_async_copy(chan_out, w2, wsem.at[1])
    wcopy1.start()
    wcopy2.start()

    barrier = pltpu.get_barrier_semaphore()
    for dev in ((dp, xp), (dp, diag), dev_sib, dev_y, dev_za, dev_zb):
        pl.semaphore_signal(barrier, inc=1, device_id=dev, device_id_type=MESH)
    pl.semaphore_wait(barrier, 6)

    def gather_copy(src, dst, ssem, rsem, i, q):
        return pltpu.make_async_remote_copy(
            src_ref=src.at[q * ni + i],
            dst_ref=dst.at[i, me],
            send_sem=ssem.at[i, q],
            recv_sem=rsem.at[i, me],
            device_id=(dp, q),
            device_id_type=MESH,
        )

    def gather_from(src, dst, ssem, rsem, i, q):
        return pltpu.make_async_remote_copy(
            src_ref=src.at[q * ni + i],
            dst_ref=dst.at[i, q],
            send_sem=ssem.at[i, q],
            recv_sem=rsem.at[i, q],
            device_id=(dp, q),
            device_id_type=MESH,
        )

    def gather_own(src, dst, rsem, i):
        return pltpu.make_async_copy(src.at[me * ni + i], dst.at[i, me], rsem.at[i, me])

    def return_copy(src, dst, ssem, rsem, i, q):
        return pltpu.make_async_remote_copy(
            src_ref=src.at[i, q],
            dst_ref=dst.at[me * ni + i],
            send_sem=ssem.at[i, q],
            recv_sem=rsem.at[i, me],
            device_id=(dp, q),
            device_id_type=MESH,
        )

    def return_from(src, dst, ssem, rsem, i, q):
        return pltpu.make_async_remote_copy(
            src_ref=src.at[i, q],
            dst_ref=dst.at[q * ni + i],
            send_sem=ssem.at[i, q],
            recv_sem=rsem.at[i, q],
            device_id=(dp, q),
            device_id_type=MESH,
        )

    def return_own(src, dst, ssem, i):
        return pltpu.make_async_copy(src.at[i, me], dst.at[me * ni + i], ssem.at[i, me])

    def each_image(fn):
        def body(i, carry):
            fn(i)
            return carry

        lax.fori_loop(0, ni, body, 0)

    def send_patches(i):
        for q in peers:
            gather_copy(patches, xin, xs_s, xs_r, i, q).start()
        gather_own(patches, xin, xs_r, i).start()

    each_image(send_patches)

    rows32[...] = jnp.zeros_like(rows32)
    for w_in, w_row, w_col in ((tok_in, tin, tin_t), (tok_out_t, tout_t, tout)):
        wide = w_in[...].astype(F32)
        rows32[:, :ds] = jnp.zeros((rows, ds), F32)
        for s in range(4):
            rows32[s * SLAB : s * SLAB + part, :ds] = wide[s * part : (s + 1) * part]
        full = rows32[:, :ds]
        w_row[...] = full.astype(BF16)
        w_col[...] = full.T.astype(BF16)
    rows32[...] = jnp.zeros_like(rows32)
    d_tin[...] = jnp.zeros_like(d_tin)
    d_tout[...] = jnp.zeros_like(d_tout)
    vecs[...] = jnp.zeros_like(vecs)
    d_tb[...] = jnp.zeros_like(d_tb)

    def widen_rows(ref, i):
        for s in range(4):
            rows32[s * SLAB : s * SLAB + part, :] = ref[i, s].astype(F32)
        return rows32[...]

    def image_rows(i):
        return pl.ds(pl.multiple_of(i * rows, rows), rows)

    wcopy1.wait()
    wcopy2.wait()

    def forward(i):
        for q in peers:
            gather_from(patches, xin, xs_s, xs_r, i, q).wait_recv()
        gather_own(patches, xin, xs_r, i).wait()
        for q in peers:
            gather_copy(out_grad, uin, us_s, us_r, i, q).start()
        gather_own(out_grad, uin, us_r, i).start()
        at = image_rows(i)
        x = widen_rows(xin, i)
        xh, _ = normalise(x)
        normed = (xh * gain_one[...] + shift_one[...]).astype(BF16)
        hidden = gelu(dot(tin_t[...], normed) + tok_inbias[...]).astype(BF16)
        mixed = (dot(tout_t[...], hidden) + tok_outbias[...]).astype(BF16)
        mixed_keep[at, :] = mixed
        middle = x + mixed.astype(F32)
        xh, _ = normalise(middle)
        second = xh * gain_two[...] + shift_two[...]
        sec[at, :] = second.astype(BF16)
        sec_t[:, at] = second.T.astype(BF16)
        gsec[at, :] = middle + chan_outbias[...]

        def hidden_block(c, carry):
            cs = pl.ds(pl.multiple_of(c * 768, 768), 768)
            activ = gelu(dot(sec[at, :], w1[:, cs]) + chan_inbias[:, cs]).astype(BF16)
            gsec[at, :] += dot(activ, w2[cs, :])
            return carry

        lax.fori_loop(0, dc // 768, hidden_block, 0)
        for s in range(4):
            base = pl.multiple_of(i * rows, rows) + s * SLAB
            mo[i, s] = gsec[pl.ds(base, SLAB), :][:part].astype(BF16)

    each_image(forward)

    def take_upstream(i):
        for q in peers:
            gather_from(out_grad, uin, us_s, us_r, i, q).wait_recv()
        gather_own(out_grad, uin, us_r, i).wait()
        for q in peers:
            return_copy(mo, mixed_out, ms_s, ms_r, i, q).start()
        return_own(mo, mixed_out, ms_s, i).start()
        at = image_rows(i)
        up = widen_rows(uin, i)
        up = jnp.where(me * ni + i < valid[0], up, 0.0)
        ups[at, :] = up.astype(BF16)
        ups_t[:, at] = up.T.astype(BF16)
        vecs[4:5, :] += jnp.sum(up, axis=0, keepdims=True)

    each_image(take_upstream)

    gsec[...] = jnp.zeros_like(gsec)

    def chunk_compute(c):
        cs = pl.ds(pl.multiple_of(c * FC, FC), FC)
        activ, slope = gelu_and_slope(dot(sec[...], w1[:, cs]) + chan_inbias[:, cs])
        act_s[...] = activ.astype(BF16)
        gi = (dot_nt(ups[...], w2[cs, :]) * slope).astype(BF16)
        gi_s[...] = gi
        d_b1[:, cs] = jnp.sum(gi.astype(F32), axis=0, keepdims=True)
        gsec[...] += dot_nt(gi_s[...], w1[:, cs])
        blk[c, 0] = dot(sec_t[...], gi_s[...]).astype(BF16)
        blk[c, 1] = dot(ups_t[...], act_s[...]).astype(BF16)

    def image_backward(i):
        for q in peers:
            return_copy(mo, mixed_out, ms_s, ms_r, i, q).wait_send()
        return_own(mo, mixed_out, ms_s, i).wait()
        at = image_rows(i)
        x = widen_rows(xin, i)
        xh, r = normalise(x + mixed_keep[at, :].astype(F32))
        gs = gsec[at, :]
        vecs[2:3, :] += jnp.sum(gs * xh, axis=0, keepdims=True)
        vecs[3:4, :] += jnp.sum(gs, axis=0, keepdims=True)
        q = gs * gain_two[...]
        gm = ups[at, :].astype(F32) + r * (
            q - jnp.mean(q, axis=-1, keepdims=True) - xh * jnp.mean(q * xh, axis=-1, keepdims=True)
        )
        gmb = gm.astype(BF16)
        xh, r = normalise(x)
        normed = (xh * gain_one[...] + shift_one[...]).astype(BF16)
        hid, slope = gelu_and_slope(dot(tin_t[...], normed) + tok_inbias[...])
        gw = (dot(tout[...], gmb) * slope).astype(BF16)
        d_tout[...] += dot_nt(gmb, hid.astype(BF16))
        d_tin[...] += dot_nt(normed, gw)
        ones = jnp.ones((8, width), BF16)
        d_tb[:, :ds] += dot_nt(ones, gw)
        d_tb[:, ds : ds + rows] += dot_nt(ones, gmb)
        gn = dot(tin[...], gw).astype(BF16).astype(F32)
        vecs[0:1, :] += jnp.sum(gn * xh, axis=0, keepdims=True)
        vecs[1:2, :] += jnp.sum(gn, axis=0, keepdims=True)
        q = gn * gain_one[...]
        pg = gm + r * (
            q - jnp.mean(q, axis=-1, keepdims=True) - xh * jnp.mean(q * xh, axis=-1, keepdims=True)
        )
        for s in range(4):
            mo[i, s] = pg[s * SLAB : s * SLAB + part].astype(BF16)
        for p in peers:
            return_copy(mo, patch_grad, ps_s, ps_r, i, p).start()
        return_own(mo, patch_grad, ps_s, i).start()

    def pack_small():
        for j in range(ds // 128):
            cols = slice(j * 128, (j + 1) * 128)
            blk[nc, 0, j * rows : (j + 1) * rows, :128] = d_tin[:, cols].astype(BF16)
            blk[nc, 1, j * rows : (j + 1) * rows, :128] = d_tout[:, cols].astype(BF16)
        blk[nc, 0, :, 128:] = jnp.zeros((width, 128), BF16)
        blk[nc, 1, :, 128:] = jnp.zeros((width, 128), BF16)
        at = 0
        for v, n in (
            [(vecs[k : k + 1, :], width) for k in range(5)]
            + [(d_tb[0:1, :], ds + rows)]
            + [(d_b1[...], dc)]
        ):
            for j in range(n // 128):
                rows32[at : at + 1, :128] = v[:, j * 128 : (j + 1) * 128]
                at += 1
        up = -(-at // 16) * 16
        blk[nc, 0, :up, 128:] = rows32[:up, :128].astype(BF16)

    def stage_device(k, c):
        swap = lax.rem(c, 4) // 3
        dev1 = (dev_y[0] + swap * (dp - dev_y[0]), me + swap * (xp - me))
        dev4 = (dp + swap * (dev_y[0] - dp), xp + swap * (me - xp))
        return (dev_sib, dev1, dev_za, dev_zb, dev4, dev_zb, dev_za, dev1, dev_sib)[k]

    def stage(k, c, cc):
        swap = lax.rem(c, 4) // 3
        b1 = yb + swap * (xb - yb)
        half, quarter, eighth = width // 2, width // 4, width // 8
        o1 = b1 * half
        n1 = (1 - b1) * half
        o2 = o1 + zab * quarter
        n2 = o1 + (1 - zab) * quarter
        o3 = o2 + zbb * eighth
        n3 = o2 + (1 - zbb) * eighth
        own = blk.at[cc, core]

        def piece(start, size):
            return own.at[pl.ds(pl.multiple_of(start, 16), size), :]

        kept = (own, piece(o1, half), piece(o2, quarter), piece(o3, eighth), piece(o3, eighth))
        src = (
            blk.at[cc, 1 - core],
            piece(n1, half),
            piece(n2, quarter),
            piece(n3, eighth),
            piece(o3, eighth),
            piece(o3, eighth),
            piece(o2, quarter),
            piece(o1, half),
            own,
        )[k]
        land = (r0.at[lax.rem(cc, 4)], r1.at[cc], r2.at[cc], r3.at[cc], r4.at[cc])
        copy = pltpu.make_async_remote_copy(
            src_ref=src,
            dst_ref=land[k] if k < 5 else src,
            send_sem=as_s.at[k, cc],
            recv_sem=as_r.at[k, cc],
            device_id=stage_device(k, c),
            device_id_type=MESH,
        )
        return copy, (kept[k] if k < 5 else None), (land[k] if k < 5 else None)

    def export(cc):
        return pltpu.make_async_copy(blk.at[cc], sums.at[cc], osem.at[cc])

    def tick(t, carry):
        for k in reversed(range(9)):
            c = t - 1 - k

            @pl.when(jnp.logical_and(c >= 0, jnp.logical_or(c < nc, c == last)))
            def _(k=k, c=c):
                cc = jnp.minimum(c, nc)
                copy, kept, land = stage(k, c, cc)
                copy.wait()
                if k < 4:
                    dev = stage_device(k, c)
                    pl.semaphore_signal(free.at[k, cc], inc=1, device_id=dev, device_id_type=MESH)
                if kept is not None:
                    kept[...] = (kept[...].astype(F32) + land[...].astype(F32)).astype(BF16)
                if k < 8:
                    if k >= 4:
                        pl.semaphore_wait(free.at[7 - k, cc], 1)
                    stage(k + 1, c, cc)[0].start()
                else:
                    export(cc).start()

        @pl.when(t < nc)
        def _():
            chunk_compute(t)

        @pl.when(jnp.logical_and(t >= nc, t < last))
        def _():
            image_backward(t - nc)

        @pl.when(t == last)
        def _():
            pack_small()

        @pl.when(jnp.logical_or(t < nc, t == last))
        def _():
            stage(0, t, jnp.minimum(t, nc))[0].start()

        return carry

    lax.fori_loop(0, last + 10, tick, 0)

    def finish(i):
        for q in peers:
            gather_copy(patches, xin, xs_s, xs_r, i, q).wait_send()
            gather_copy(out_grad, uin, us_s, us_r, i, q).wait_send()
            return_from(mo, mixed_out, ms_s, ms_r, i, q).wait_recv()
            return_copy(mo, patch_grad, ps_s, ps_r, i, q).wait_send()
            return_from(mo, patch_grad, ps_s, ps_r, i, q).wait_recv()
        return_own(mo, patch_grad, ps_s, i).wait()

    each_image(finish)

    def exported(c, carry):
        export(c).wait()
        return carry

    lax.fori_loop(0, nc + 1, exported, 0)


def spread_kernel(dims, block, small, chan_in, chan_out, tok_in, tok_out_t, vecs, tok_b, b1):
    ni, part, width, ds, dc = dims
    rows = 4 * SLAB
    chan_in[...] = block[0, 0].astype(F32)
    chan_out[...] = block[0, 1].astype(F32).T

    @pl.when(pl.program_id(0) == 0)
    def _():
        for m, ref in ((0, tok_in), (1, tok_out_t)):
            for j in range(ds // 128):
                v = small[0, m, j * rows : (j + 1) * rows, :128].astype(F32)
                for s in range(4):
                    ref[s * part : (s + 1) * part, j * 128 : (j + 1) * 128] = v[
                        s * SLAB : s * SLAB + part
                    ]
        v = small[0, 0, :rows, 128:].astype(F32)
        at = 0
        for k in range(5):
            for j in range(width // 128):
                vecs[k : k + 1, j * 128 : (j + 1) * 128] = v[at : at + 1]
                at += 1
        for j in range((ds + rows) // 128):
            tok_b[:, j * 128 : (j + 1) * 128] = v[at : at + 1]
            at += 1
        for j in range(dc // 128):
            b1[:, j * 128 : (j + 1) * 128] = v[at : at + 1]
            at += 1


def slab_rows(vector, part):
    return jnp.pad(vector.reshape(4, part), ((0, 0), (0, SLAB - part))).reshape(4 * SLAB, 1)


def shards(
    mesh_shape,
    patches,
    valid_counts,
    gain_one,
    shift_one,
    tok_in,
    tok_inbias,
    tok_out,
    tok_outbias,
    gain_two,
    shift_two,
    chan_in,
    chan_inbias,
    chan_out,
    chan_outbias,
    out_grad,
):
    images, part, width = patches.shape
    s_all, ds = tok_in.shape
    dc = chan_in.shape[1]
    ni = images // 4
    rows = 4 * SLAB
    total = ni * rows
    nc = dc // FC
    dims = (ni, part, width, ds, dc)
    anywhere = pl.BlockSpec(memory_space=pl.ANY)
    vmem = pl.BlockSpec(memory_space=pltpu.VMEM)
    dma = pltpu.SemaphoreType.DMA
    row = lambda v: v.reshape(1, -1)
    mixed_out, patch_grad, sums = pl.pallas_call(
        functools.partial(layer_kernel, dims),
        name="layer",
        out_shape=(
            jax.ShapeDtypeStruct(patches.shape, BF16),
            jax.ShapeDtypeStruct(patches.shape, BF16),
            jax.ShapeDtypeStruct((nc + 1, 2, width, FC), BF16),
        ),
        in_specs=[anywhere] * 2
        + [pl.BlockSpec(memory_space=pltpu.SMEM)]
        + [vmem] * 2
        + [anywhere] * 2
        + [vmem] * 8,
        out_specs=(anywhere,) * 3,
        scratch_shapes=[
            pltpu.VMEM((width, dc), BF16),
            pltpu.VMEM((dc, width), BF16),
            pltpu.VMEM((ni, 4, part, width), BF16),
            pltpu.VMEM((ni, 4, part, width), BF16),
            pltpu.VMEM((ni, 4, part, width), BF16),
            pltpu.VMEM((rows, width), F32),
            pltpu.VMEM((rows, ds), BF16),
            pltpu.VMEM((ds, rows), BF16),
            pltpu.VMEM((ds, rows), BF16),
            pltpu.VMEM((rows, ds), BF16),
            pltpu.VMEM((total, width), BF16),
            pltpu.VMEM((total, width), BF16),
            pltpu.VMEM((width, total), BF16),
            pltpu.VMEM((total, width), BF16),
            pltpu.VMEM((width, total), BF16),
            pltpu.VMEM((total, width), F32),
            pltpu.VMEM((total, FC), BF16),
            pltpu.VMEM((total, FC), BF16),
            pltpu.VMEM((rows, ds), F32),
            pltpu.VMEM((rows, ds), F32),
            pltpu.VMEM((8, width), F32),
            pltpu.VMEM((1, dc), F32),
            pltpu.VMEM((8, ds + rows), F32),
            pltpu.VMEM((nc + 1, 2, width, FC), BF16),
            pltpu.VMEM((4, width, FC), BF16),
            pltpu.VMEM((nc + 1, width // 2, FC), BF16),
            pltpu.VMEM((nc + 1, width // 4, FC), BF16),
            pltpu.VMEM((nc + 1, width // 8, FC), BF16),
            pltpu.VMEM((nc + 1, width // 8, FC), BF16),
            dma((2,)),
            dma((nc + 1,)),
        ]
        + [dma((ni, 4))] * 8
        + [dma((9, nc + 1))] * 2
        + [pltpu.SemaphoreType.REGULAR((4, nc + 1))],
        compiler_params=pltpu.CompilerParams(
            collective_id=0, has_side_effects=True, vmem_limit_bytes=63 << 20
        ),
        cost_estimate=pl.CostEstimate(
            flops=14 * total * width * dc,
            bytes_accessed=40 << 20,
            transcendentals=total * dc,
        ),
    )(
        patches,
        out_grad,
        valid_counts,
        tok_in,
        tok_out.T,
        chan_in,
        chan_out,
        row(gain_one),
        row(shift_one),
        row(gain_two),
        row(shift_two),
        tok_inbias.reshape(ds, 1),
        slab_rows(tok_outbias, part),
        row(chan_inbias),
        row(chan_outbias),
    )
    g_chan_in, g_chan_out, g_tok_in, g_tok_out_t, vecs, tok_b, b1 = pl.pallas_call(
        functools.partial(spread_kernel, dims),
        name="spread",
        grid=(nc,),
        out_shape=(
            jax.ShapeDtypeStruct((width, dc), F32),
            jax.ShapeDtypeStruct((dc, width), F32),
            jax.ShapeDtypeStruct((s_all, ds), F32),
            jax.ShapeDtypeStruct((s_all, ds), F32),
            jax.ShapeDtypeStruct((5, width), F32),
            jax.ShapeDtypeStruct((1, ds + rows), F32),
            jax.ShapeDtypeStruct((1, dc), F32),
        ),
        in_specs=[
            pl.BlockSpec((1, 2, width, FC), lambda c: (c, 0, 0, 0)),
            pl.BlockSpec((1, 2, width, FC), lambda c: (nc, 0, 0, 0)),
        ],
        out_specs=(
            pl.BlockSpec((width, FC), lambda c: (0, c)),
            pl.BlockSpec((FC, width), lambda c: (c, 0)),
            pl.BlockSpec((s_all, ds), lambda c: (0, 0)),
            pl.BlockSpec((s_all, ds), lambda c: (0, 0)),
            pl.BlockSpec((5, width), lambda c: (0, 0)),
            pl.BlockSpec((1, ds + rows), lambda c: (0, 0)),
            pl.BlockSpec((1, dc), lambda c: (0, 0)),
        ),
        compiler_params=pltpu.CompilerParams(vmem_limit_bytes=32 << 20),
    )(sums, sums)
    grads = (
        vecs[0],
        vecs[1],
        g_tok_in,
        tok_b[0, :ds],
        g_tok_out_t.T,
        tok_b[0, ds:].reshape(4, SLAB)[:, :part].reshape(s_all),
        vecs[2],
        vecs[3],
        g_chan_in,
        b1[0],
        g_chan_out,
        vecs[4],
    )
    if mesh_shape["dp"] > GROUP:
        count = mesh_shape["dp"] // GROUP
        groups = [[g * GROUP + j for g in range(count)] for j in range(GROUP)]
        grads = lax.psum(grads, "dp", axis_index_groups=groups)
    return (mixed_out, patch_grad) + grads


def solution(mesh):
    whole, split = P(), P("dp", "mix", None)
    return jax.shard_map(
        functools.partial(shards, dict(mesh.shape)),
        mesh=mesh,
        in_specs=(split, P("dp")) + (whole,) * 12 + (split,),
        out_specs=(split, split) + (whole,) * 12,
        check_vma=False,
    )
```

time: 731 us -> 256 us (0.35)
  waiting for transfers between devices: 239 us -> 0 us
  Pallas kernels: 0 us -> 235 us
  local copies, waits for them, and re-layouts: 220 us -> 19.2 us
  matrix products: 117 us -> 0 us
  blocking collectives: 73.5 us -> 0 us
  other arithmetic: 44.7 us -> 0 us
  between operations: 15.3 us -> 1.32 us
  starting transfers between devices: 13.2 us -> 0 us
    pallas_call x0 -> x2, Pallas kernels: none -> 235 us  [the longest x1 227 us: shards(): pl.pallas_call(functools.partial(layer_kernel, dims), name='layer', out_s...]
    psum x1 -> x0, waiting for transfers between devices: 155 us -> none  [shards(): lax.psum((grad_gain_one, grad_shift_one, grad_tok_in, grad_tok_inbias, gr...]
    dot_general x12 -> x0, matrix products: 117 us -> none  [the longest x1 19.9 us: shards(): jnp.einsum('rc,fc->rf', upstream, chan_out, preferred_element_type=jnp.fl...]
    convert_element_type x12 -> x0, local copies, waits for them, and re-layouts: 90.6 us -> none  [the longest x4 27.2 us: shards(): middle = inputs + mixed.astype(jnp.float32)]
    all_to_all x3 -> x0, waiting for transfers between devices: 84.3 us -> none  [the longest x1 55.7 us: shards(): lax.all_to_all(grad_columns, 'mix', split_axis=1, concat_axis=2, tiled=True)]
    unnamed x86 -> x8, local copies, waits for them, and re-layouts: 71.9 us -> 7.87 us
    psum x1 -> x0, blocking collectives: 42.5 us -> none  [shards(): lax.psum((grad_gain_one, grad_shift_one, grad_tok_in, grad_tok_inbias, gr...]
    all_to_all x6 -> x0, local copies, waits for them, and re-layouts: 41.3 us -> none  [the longest x2 15.3 us: shards(): lax.all_to_all(normed, 'mix', split_axis=2, concat_axis=1, tiled=True)]
  transfers between devices with their start and end apart: 4 -> 0, of which waited for: 3 -> 0; matrix products, arithmetic and copies ran while one was open for 13% -> 0% of each run, Pallas kernels for 0% -> 0%
where the time goes in v1:
time: 256 us
  Pallas kernels  235 us (92%)
  local copies, waits for them, and re-layouts  19.2 us (8%)
    pallas_call x1, Pallas kernels, shards(): pl.pallas_call(functools.partial(layer_kernel, dims), name='layer', out_s...  227 us
    pallas_call x1, Pallas kernels, shards(): pl.pallas_call(functools.partial(spread_kernel, dims), name='spread', gri...  8.52 us
    unnamed x8, local copies, waits for them, and re-layouts  7.87 us
    reshape x5, local copies, waits for them, and re-layouts, shards(): row = lambda v: v.reshape(1, -1)  6.33 us

profile of v1, /device:TPU:0, one launch (start us, length us, event | category | flops | bytes accessed | tf_op | source)
XLA Modules:
  0.0 255.6 jit_solution(12783573160311520450)
XLA Ops:
  1.3 0.8 reshape.63
  2.1 1.3 reshape.58.gain_one
  3.3 1.3 reshape.59.shift_one
  4.6 1.3 reshape.60.gain_two
  5.9 1.3 reshape.61.shift_two
  7.1 1.3 reshape.66.chan_outbias
  8.4 0.8 reshape.69.tok_outbias
  9.2 1.5 reshape.68.tok_inbias
  10.7 226.5 %layer.1 = (bf16[28,49,768]{2,1,0:T(8,128)(2,1)}, bf16[28,49,768]{2,1,0:T(8,128)(2,1)}, bf16[13,2,768,256]{3,2,1,0:T(8,128)(2,1)}) custom-call(bf16[28,49,768]{2,1,0:T(8,128)(2,1)} %patches.1, bf16[28,49,768]{2,1,0:T(8,128)(2,1)} %out_grad.1, s32[1]{0:T(128)S(6)} %copy.33.valid, bf16[196,384]{1,0:T(8,128)(2,1)} %tok_in.1, bf16[196,384]{1,0:T(8,128)(2,1)} %bitcast.7, ...), custom_call_target="tpu_custom_call" | custom-call | flops 59190018048 | bytes 41943040 | tf_op jit(solution)/shard_map/layer/pallas_call | solution.py:520
  237.2 0.0 copy-start
  237.2 3.9 %copy-done = bf16[13,2,768,256]{3,2,1,0:T(8,128)(2,1)S(1)} copy-done((bf16[13,2,768,256]{3,2,1,0:T(8,128)(2,1)S(1)}, bf16[13,2,768,256]{3,2,1,0:T(8,128)(2,1)}, u32[]{:S(2)}) %copy-start) | copy-done | bytes 10223640
  241.1 0.0 copy-start.2
  241.1 8.5 %spread.1 = (f32[768,3072]{1,0:T(8,128)}, f32[3072,768]{1,0:T(8,128)}, f32[196,384]{1,0:T(8,128)}, f32[196,384]{1,0:T(8,128)}, f32[5,768]{1,0:T(8,128)S(1)}, /*index=5*/f32[1,640]{1,0:T(1,128)S(1)}, f32[1,3072]{1,0:T(1,128)}) custom-call(bf16[13,2,768,256]{3,2,1,0:T(8,128)(2,1)S(1)} %copy-done, bf16[13,2,768,256]{3,2,1,0:T(8,128)(2,1)S(1)} %copy-done), custom_call_target="tpu_custom_call" | custom-call | tf_op jit(solution)/shard_map/spread/pallas_call | solution.py:595
  249.6 0.6 slice_reduce_fusion
  250.3 0.6 slice_reduce_fusion.5
  250.9 0.1 reshape_squeeze.3
  251.0 0.6 reshape.67
  251.6 0.0 copy-done.2
  251.6 0.0 copy-start.1
  251.6 1.4 copy.34
  253.0 1.1 copy-done.1
  254.2 1.4 copy.35
  (2 shorter events, 0.0 us)
Async XLA Ops:
  237.2 3.9 %copy-start = (bf16[13,2,768,256]{3,2,1,0:T(8,128)(2,1)S(1)}, bf16[13,2,768,256]{3,2,1,0:T(8,128)(2,1)}, u32[]{:S(2)}) copy-start(bf16[13,2,768,256]{3,2,1,0:T(8,128)(2,1)} %get-tuple-element.26.block.small) | copy-start | bytes 30670852
  241.1 10.5 %copy-start.2 = (bf16[28,49,768]{2,1,0:T(8,128)(2,1)S(1)}, bf16[28,49,768]{2,1,0:T(8,128)(2,1)}, u32[]{:S(2)}) copy-start(bf16[28,49,768]{2,1,0:T(8,128)(2,1)} %get-tuple-element.53) | copy-start | bytes 6322180
  251.6 2.5 copy-start.1

commit v2 on v1

--- a/solution.py
+++ b/solution.py
@@ -11,6 +11,7 @@
 SQ = 0.7978845608028654
 CU = 0.044715
 GROUP = 8
+WAIT = (2, 4, 6, 7, 8, 9, 11, 13, 14)
 SLAB = 64
 FC = 256
 NT = (((1,), (1,)), ((), ()))
@@ -58,14 +59,14 @@
     tok_out_t,
     chan_in,
     chan_out,
-    gain_one,
-    shift_one,
-    gain_two,
-    shift_two,
-    tok_inbias,
-    tok_outbias,
+    gain_one_flat,
+    shift_one_flat,
+    gain_two_flat,
+    shift_two_flat,
+    tok_inbias_flat,
+    tok_outbias_flat,
     chan_inbias,
-    chan_outbias,
+    chan_outbias_flat,
     mixed_out,
     patch_grad,
     sums,
@@ -92,6 +93,13 @@
     vecs,
     d_b1,
     d_tb,
+    gain_one,
+    shift_one,
+    gain_two,
+    shift_two,
+    chan_outbias,
+    tok_inbias,
+    tok_outbias,
     blk,
     r0,
     r1,
@@ -115,7 +123,6 @@
     ni, part, width, ds, dc = dims
     nc = dc // FC
     rows = 4 * SLAB
-    last = nc + ni
     me = lax.axis_index("mix")
     dp = lax.axis_index("dp")
     core = lax.rem(me, 2)
@@ -212,6 +219,22 @@
         full = rows32[:, :ds]
         w_row[...] = full.astype(BF16)
         w_col[...] = full.T.astype(BF16)
+    for flat, row in (
+        (gain_one_flat, gain_one),
+        (shift_one_flat, shift_one),
+        (gain_two_flat, gain_two),
+        (shift_two_flat, shift_two),
+        (chan_outbias_flat, chan_outbias),
+    ):
+        row[...] = flat[...].reshape(1, width)
+    tok_inbias[...] = jnp.broadcast_to(tok_inbias_flat[...].reshape(1, ds), (8, ds)).T[:, :1]
+    rows32[...] = jnp.zeros_like(rows32)
+    rows32[:1, : 4 * part] = tok_outbias_flat[...].reshape(1, 4 * part)
+    column = rows32[:8, :rows].T
+    rows32[...] = jnp.zeros_like(rows32)
+    for s in range(4):
+        rows32[s * SLAB : s * SLAB + part, :8] = column[s * part : (s + 1) * part]
+    tok_outbias[...] = rows32[:, :1]
     rows32[...] = jnp.zeros_like(rows32)
     d_tin[...] = jnp.zeros_like(d_tin)
     d_tout[...] = jnp.zeros_like(d_tout)
@@ -256,20 +279,15 @@
             gsec[at, :] += dot(activ, w2[cs, :])
             return carry
 
-        lax.fori_loop(0, dc // 768, hidden_block, 0)
+        lax.fori_loop(0, dc // 768, hidden_block, 0, unroll=True)
         for s in range(4):
             base = pl.multiple_of(i * rows, rows) + s * SLAB
             mo[i, s] = gsec[pl.ds(base, SLAB), :][:part].astype(BF16)
-
-    each_image(forward)
 
     def take_upstream(i):
         for q in peers:
             gather_from(out_grad, uin, us_s, us_r, i, q).wait_recv()
         gather_own(out_grad, uin, us_r, i).wait()
-        for q in peers:
-            return_copy(mo, mixed_out, ms_s, ms_r, i, q).start()
-        return_own(mo, mixed_out, ms_s, i).start()
         at = image_rows(i)
         up = widen_rows(uin, i)
         up = jnp.where(me * ni + i < valid[0], up, 0.0)
@@ -277,7 +295,27 @@
         ups_t[:, at] = up.T.astype(BF16)
         vecs[4:5, :] += jnp.sum(up, axis=0, keepdims=True)
 
-    each_image(take_upstream)
+    late = min(3, ni)
+
+    def arrive(i):
+        @pl.when(i < ni)
+        def _():
+            forward(i)
+
+        @pl.when(i >= late)
+        def _():
+            take_upstream(i - late)
+
+    def arrive_step(i, carry):
+        arrive(i)
+        return carry
+
+    lax.fori_loop(0, ni + late, arrive_step, 0)
+
+    def send_mixed(i):
+        for q in peers:
+            return_copy(mo, mixed_out, ms_s, ms_r, i, q).start()
+        return_own(mo, mixed_out, ms_s, i).start()
 
     gsec[...] = jnp.zeros_like(gsec)
 
@@ -354,7 +392,7 @@
         dev4 = (dp + swap * (dev_y[0] - dp), xp + swap * (me - xp))
         return (dev_sib, dev1, dev_za, dev_zb, dev4, dev_zb, dev_za, dev1, dev_sib)[k]
 
-    def stage(k, c, cc):
+    def stage(k, c):
         swap = lax.rem(c, 4) // 3
         b1 = yb + swap * (xb - yb)
         half, quarter, eighth = width // 2, width // 4, width // 8
@@ -364,14 +402,14 @@
         n2 = o1 + (1 - zab) * quarter
         o3 = o2 + zbb * eighth
         n3 = o2 + (1 - zbb) * eighth
-        own = blk.at[cc, core]
+        own = blk.at[c, core]
 
         def piece(start, size):
             return own.at[pl.ds(pl.multiple_of(start, 16), size), :]
 
         kept = (own, piece(o1, half), piece(o2, quarter), piece(o3, eighth), piece(o3, eighth))
         src = (
-            blk.at[cc, 1 - core],
+            blk.at[c, 1 - core],
             piece(n1, half),
             piece(n2, quarter),
             piece(n3, eighth),
@@ -381,60 +419,74 @@
             piece(o1, half),
             own,
         )[k]
-        land = (r0.at[lax.rem(cc, 4)], r1.at[cc], r2.at[cc], r3.at[cc], r4.at[cc])
+        land = (r0.at[lax.rem(c, 4)], r1.at[c], r2.at[c], r3.at[c], r4.at[c])
         copy = pltpu.make_async_remote_copy(
             src_ref=src,
             dst_ref=land[k] if k < 5 else src,
-            send_sem=as_s.at[k, cc],
-            recv_sem=as_r.at[k, cc],
+            send_sem=as_s.at[k, c],
+            recv_sem=as_r.at[k, c],
             device_id=stage_device(k, c),
             device_id_type=MESH,
         )
         return copy, (kept[k] if k < 5 else None), (land[k] if k < 5 else None)
 
-    def export(cc):
-        return pltpu.make_async_copy(blk.at[cc], sums.at[cc], osem.at[cc])
-
-    def tick(t, carry):
+    def export(c):
+        return pltpu.make_async_copy(blk.at[c], sums.at[c], osem.at[c])
+
+    def step(u, carry):
         for k in reversed(range(9)):
-            c = t - 1 - k
-
-            @pl.when(jnp.logical_and(c >= 0, jnp.logical_or(c < nc, c == last)))
+            c = u - WAIT[k]
+
+            @pl.when(jnp.logical_and(c >= 0, c <= nc))
             def _(k=k, c=c):
-                cc = jnp.minimum(c, nc)
-                copy, kept, land = stage(k, c, cc)
+                copy, kept, land = stage(k, c)
                 copy.wait()
                 if k < 4:
                     dev = stage_device(k, c)
-                    pl.semaphore_signal(free.at[k, cc], inc=1, device_id=dev, device_id_type=MESH)
+                    pl.semaphore_signal(free.at[k, c], inc=1, device_id=dev, device_id_type=MESH)
                 if kept is not None:
                     kept[...] = (kept[...].astype(F32) + land[...].astype(F32)).astype(BF16)
                 if k < 8:
                     if k >= 4:
-                        pl.semaphore_wait(free.at[7 - k, cc], 1)
-                    stage(k + 1, c, cc)[0].start()
+                        pl.semaphore_wait(free.at[7 - k, c], 1)
+                    stage(k + 1, c)[0].start()
                 else:
-                    export(cc).start()
-
-        @pl.when(t < nc)
+                    export(c).start()
+
+        @pl.when(u < ni)
         def _():
-            chunk_compute(t)
-
-        @pl.when(jnp.logical_and(t >= nc, t < last))
+            send_mixed(u)
+
+        @pl.when(u <= nc)
         def _():
-            image_backward(t - nc)
-
-        @pl.when(t == last)
-        def _():
-            pack_small()
-
-        @pl.when(jnp.logical_or(t < nc, t == last))
-        def _():
-            stage(0, t, jnp.minimum(t, nc))[0].start()
+            def quantum(w, carry):
+                @pl.when(w < nc)
+                def _():
+                    chunk_compute(w)
+
+                @pl.when(w >= nc)
+                def _():
+                    image_backward(w - nc)
+
+                return carry
+
+            lead = nc // 2
+
+            def done(n):
+                rest = jnp.maximum(n - lead, 0) * (nc + ni - lead) // (nc + 1 - lead)
+                return jnp.minimum(n, lead) + rest
+
+            lax.fori_loop(done(u), done(u + 1), quantum, 0)
+
+            @pl.when(u == nc)
+            def _():
+                pack_small()
+
+            stage(0, u)[0].start()
 
         return carry
 
-    lax.fori_loop(0, last + 10, tick, 0)
+    lax.fori_loop(0, nc + 1 + WAIT[-1], step, 0)
 
     def finish(i):
         for q in peers:
@@ -454,9 +506,56 @@
     lax.fori_loop(0, nc + 1, exported, 0)
 
 
-def spread_kernel(dims, block, small, chan_in, chan_out, tok_in, tok_out_t, vecs, tok_b, b1):
+def spread_kernel(
+    dims,
+    block,
+    small,
+    mixed_from,
+    patch_from,
+    chan_in,
+    chan_out,
+    tok_in,
+    tok_out_t,
+    gain_one,
+    shift_one,
+    tok_inbias,
+    tok_outbias,
+    gain_two,
+    shift_two,
+    chan_inbias,
+    chan_outbias,
+    mixed_to,
+    patch_to,
+    hold,
+    sem,
+):
     ni, part, width, ds, dc = dims
     rows = 4 * SLAB
+    loads = (
+        pltpu.make_async_copy(mixed_from, hold.at[0], sem.at[0]),
+        pltpu.make_async_copy(patch_from, hold.at[1], sem.at[1]),
+    )
+    stores = (
+        pltpu.make_async_copy(hold.at[0], mixed_to, sem.at[2]),
+        pltpu.make_async_copy(hold.at[1], patch_to, sem.at[3]),
+    )
+
+    @pl.when(pl.program_id(0) == 0)
+    def _():
+        for copy in loads:
+            copy.start()
+
+    @pl.when(pl.program_id(0) == 3)
+    def _():
+        for load, store in zip(loads, stores):
+            load.wait()
+            store.start()
+
+    @pl.when(pl.program_id(0) == pl.num_programs(0) - 1)
+    def _():
+        for store in stores:
+            store.wait()
+
     chan_in[...] = block[0, 0].astype(F32)
     chan_out[...] = block[0, 1].astype(F32).T
 
@@ -471,20 +570,23 @@
                     ]
         v = small[0, 0, :rows, 128:].astype(F32)
         at = 0
-        for k in range(5):
-            for j in range(width // 128):
-                vecs[k : k + 1, j * 128 : (j + 1) * 128] = v[at : at + 1]
-                at += 1
-        for j in range((ds + rows) // 128):
-            tok_b[:, j * 128 : (j + 1) * 128] = v[at : at + 1]
-            at += 1
-        for j in range(dc // 128):
-            b1[:, j * 128 : (j + 1) * 128] = v[at : at + 1]
-            at += 1
-
-
-def slab_rows(vector, part):
-    return jnp.pad(vector.reshape(4, part), ((0, 0), (0, SLAB - part))).reshape(4 * SLAB, 1)
+        for ref, n in (
+            (gain_one, width),
+            (shift_one, width),
+            (gain_two, width),
+            (shift_two, width),
+            (chan_outbias, width),
+            (tok_inbias, ds),
+            (tok_outbias, rows),
+            (chan_inbias, dc),
+        ):
+            flat = jnp.concatenate([v[at + j : at + j + 1] for j in range(n // 128)], axis=1)
+            at += n // 128
+            if ref is tok_outbias:
+                flat = jnp.concatenate(
+                    [flat[:, s * SLAB : s * SLAB + part] for s in range(4)], axis=1
+                )
+            ref[...] = flat.reshape(ref.shape)
 
 
 def shards(
@@ -516,8 +618,7 @@
     anywhere = pl.BlockSpec(memory_space=pl.ANY)
     vmem = pl.BlockSpec(memory_space=pltpu.VMEM)
     dma = pltpu.SemaphoreType.DMA
-    row = lambda v: v.reshape(1, -1)
-    mixed_out, patch_grad, sums = pl.pallas_call(
+    mixed_here, patch_here, sums = pl.pallas_call(
         functools.partial(layer_kernel, dims),
         name="layer",
         out_shape=(
@@ -555,6 +656,13 @@
             pltpu.VMEM((8, width), F32),
             pltpu.VMEM((1, dc), F32),
             pltpu.VMEM((8, ds + rows), F32),
+            pltpu.VMEM((1, width), F32),
+            pltpu.VMEM((1, width), F32),
+            pltpu.VMEM((1, width), F32),
+            pltpu.VMEM((1, width), F32),
+            pltpu.VMEM((1, width), F32),
+            pltpu.VMEM((ds, 1), F32),
+            pltpu.VMEM((rows, 1), F32),
             pltpu.VMEM((nc + 1, 2, width, FC), BF16),
             pltpu.VMEM((4, width, FC), BF16),
             pltpu.VMEM((nc + 1, width // 2, FC), BF16),
@@ -583,16 +691,18 @@
         tok_out.T,
         chan_in,
         chan_out,
-        row(gain_one),
-        row(shift_one),
-        row(gain_two),
-        row(shift_two),
-        tok_inbias.reshape(ds, 1),
-        slab_rows(tok_outbias, part),
-        row(chan_inbias),
-        row(chan_outbias),
+        gain_one,
+        shift_one,
+        gain_two,
+        shift_two,
+        tok_inbias,
+        tok_outbias,
+        chan_inbias.reshape(1, dc),
+        chan_outbias,
     )
-    g_chan_in, g_chan_out, g_tok_in, g_tok_out_t, vecs, tok_b, b1 = pl.pallas_call(
+    vec = lambda n: (jax.ShapeDtypeStruct((n,), F32), pl.BlockSpec((n,), lambda c: (0,)))
+    vectors = [vec(n) for n in (width, width, ds, s_all, width, width, dc, width)]
+    out = pl.pallas_call(
         functools.partial(spread_kernel, dims),
         name="spread",
         grid=(nc,),
@@ -601,38 +711,44 @@
             jax.ShapeDtypeStruct((dc, width), F32),
             jax.ShapeDtypeStruct((s_all, ds), F32),
             jax.ShapeDtypeStruct((s_all, ds), F32),
-            jax.ShapeDtypeStruct((5, width), F32),
-            jax.ShapeDtypeStruct((1, ds + rows), F32),
-            jax.ShapeDtypeStruct((1, dc), F32),
+        )
+        + tuple(v[0] for v in vectors)
+        + (
+            jax.ShapeDtypeStruct(patches.shape, BF16),
+            jax.ShapeDtypeStruct(patches.shape, BF16),
         ),
         in_specs=[
             pl.BlockSpec((1, 2, width, FC), lambda c: (c, 0, 0, 0)),
             pl.BlockSpec((1, 2, width, FC), lambda c: (nc, 0, 0, 0)),
+            anywhere,
+            anywhere,
         ],
         out_specs=(
             pl.BlockSpec((width, FC), lambda c: (0, c)),
             pl.BlockSpec((FC, width), lambda c: (c, 0)),
             pl.BlockSpec((s_all, ds), lambda c: (0, 0)),
             pl.BlockSpec((s_all, ds), lambda c: (0, 0)),
-            pl.BlockSpec((5, width), lambda c: (0, 0)),
-            pl.BlockSpec((1, ds + rows), lambda c: (0, 0)),
-            pl.BlockSpec((1, dc), lambda c: (0, 0)),
-        ),
-        compiler_params=pltpu.CompilerParams(vmem_limit_bytes=32 << 20),
-    )(sums, sums)
+        )
+        + tuple(v[1] for v in vectors)
+        + (anywhere, anywhere),
+        scratch_shapes=[pltpu.VMEM((2,) + patches.shape, BF16), dma((4,))],
+        compiler_params=pltpu.CompilerParams(vmem_limit_bytes=63 << 20),
+    )(sums, sums, mixed_here, patch_here)
+    g_chan_in, g_chan_out, g_tok_in, g_tok_out_t = out[:4]
+    g_one, s_one, b_tin, b_tout, g_two, s_two, b_cin, b_cout, mixed_out, patch_grad = out[4:]
     grads = (
-        vecs[0],
-        vecs[1],
+        g_one,
+        s_one,
         g_tok_in,
-        tok_b[0, :ds],
+        b_tin,
         g_tok_out_t.T,
-        tok_b[0, ds:].reshape(4, SLAB)[:, :part].reshape(s_all),
-        vecs[2],
-        vecs[3],
+        b_tout,
+        g_two,
+        s_two,
         g_chan_in,
-        b1[0],
+        b_cin,
         g_chan_out,
-        vecs[4],
+        b_cout,
     )
     if mesh_shape["dp"] > GROUP:
         count = mesh_shape["dp"] // GROUP

time: 256 us -> 221 us (0.86)
  local copies, waits for them, and re-layouts: 19.2 us -> 0 us
  Pallas kernels: 235 us -> 219 us
    pallas_call x1, Pallas kernels: 227 us -> 203 us  [shards(): pl.pallas_call(functools.partial(layer_kernel, dims), name='layer', out_s...]
    reshape x9 -> x0, local copies, waits for them, and re-layouts: 10 us -> none  [the longest x5 6.33 us: shards(): row = lambda v: v.reshape(1, -1)]
    pallas_call x1, Pallas kernels: 8.52 us -> 16.7 us  [shards(): pl.pallas_call(functools.partial(spread_kernel, dims), name='spread', gri...]
    unnamed x8 -> x0, local copies, waits for them, and re-layouts: 7.87 us -> none
where the time goes in v2:
time: 221 us
  Pallas kernels  219 us (99%)
    pallas_call x1, Pallas kernels, shards(): pl.pallas_call(functools.partial(layer_kernel, dims), name='layer', out_s...  203 us
    pallas_call x1, Pallas kernels, shards(): pl.pallas_call(functools.partial(spread_kernel, dims), name='spread', gri...  16.7 us

profile of v2, /device:TPU:0, one launch (start us, length us, event | category | flops | bytes accessed | tf_op | source)
XLA Modules:
  0.0 220.5 jit_solution(14986301483231403979)
XLA Ops:
  1.3 202.5 %layer.1 = (bf16[28,49,768]{2,1,0:T(8,128)(2,1)}, bf16[28,49,768]{2,1,0:T(8,128)(2,1)}, bf16[13,2,768,256]{3,2,1,0:T(8,128)(2,1)}) custom-call(bf16[28,49,768]{2,1,0:T(8,128)(2,1)} %patches.1, bf16[28,49,768]{2,1,0:T(8,128)(2,1)} %out_grad.1, s32[1]{0:T(128)S(6)} %copy.29.valid, bf16[196,384]{1,0:T(8,128)(2,1)} %tok_in.1, bf16[196,384]{1,0:T(8,128)(2,1)} %bitcast.4, ...), custom_call_target="tpu_custom_call" | custom-call | flops 59190018048 | bytes 41943040 | tf_op jit(solution)/shard_map/layer/pallas_call | solution.py:621
  203.8 16.7 %spread.1 = (f32[768,3072]{1,0:T(8,128)}, f32[3072,768]{1,0:T(8,128)}, f32[196,384]{1,0:T(8,128)}, f32[196,384]{1,0:T(8,128)}, f32[768]{0:T(1024)}, /*index=5*/f...) custom-call(bf16[13,2,768,256]{3,2,1,0:T(8,128)(2,1)} %get-tuple-ele, ...), custom_call_target="tpu_custom_call" | custom-call | tf_op jit(solution)/shard_map/spread/pallas_call | solution.py:705

commit v3 on v2

--- a/solution.py
+++ b/solution.py
@@ -11,9 +11,13 @@
 SQ = 0.7978845608028654
 CU = 0.044715
 GROUP = 8
-WAIT = (2, 4, 6, 7, 8, 9, 11, 13, 14)
+WIDE = 2
+LEAD = 8
+EXTRA = 4
+WAIT = (2, 4, 6, 8, 10, 12, 14, 17, 19)
 SLAB = 64
 FC = 256
+SPLIT = 512
 NT = (((1,), (1,)), ((), ()))
 F32 = jnp.float32
 BF16 = jnp.bfloat16
@@ -22,14 +26,13 @@
 
 def gelu_and_slope(v):
     v2 = v * v
-    t = jnp.tanh(v * (SQ + (SQ * CU) * v2))
-    h = 0.5 * v
-    return h + h * t, 0.5 + 0.5 * t + h * (1.0 - t * t) * (SQ + (3.0 * SQ * CU) * v2)
+    p = 0.5 + 0.5 * jnp.tanh(v * (SQ + (SQ * CU) * v2))
+    g = v * p
+    return g, p + g * (1.0 - p) * (2.0 * SQ + (6.0 * SQ * CU) * v2)
 
 
 def gelu(v):
-    h = 0.5 * v
-    return h + h * jnp.tanh(v * (SQ + (SQ * CU) * (v * v)))
+    return v * (0.5 + 0.5 * jnp.tanh(v * (SQ + (SQ * CU) * (v * v))))
 
 
 def normalise(v):
@@ -44,6 +47,11 @@
 
 def dot_nt(a, b):
     return lax.dot_general(a, b, NT, preferred_element_type=F32)
+
+
+def spare_row(n, part):
+    spare = SLAB - part
+    return n // spare * SLAB + part + n % spare
 
 
 def flip(index, bit, step):
@@ -319,16 +327,26 @@
 
     gsec[...] = jnp.zeros_like(gsec)
 
-    def chunk_compute(c):
-        cs = pl.ds(pl.multiple_of(c * FC, FC), FC)
-        activ, slope = gelu_and_slope(dot(sec[...], w1[:, cs]) + chan_inbias[:, cs])
-        act_s[...] = activ.astype(BF16)
-        gi = (dot_nt(ups[...], w2[cs, :]) * slope).astype(BF16)
-        gi_s[...] = gi
-        d_b1[:, cs] = jnp.sum(gi.astype(F32), axis=0, keepdims=True)
+    def chunk_compute(b):
+        cs = pl.ds(pl.multiple_of(b * FC, FC), FC)
+        total = jnp.zeros((1, FC), F32)
+        for i in range(ni):
+            at = slice(i * rows, (i + 1) * rows)
+            inner = dot(sec[at, :], w1[:, cs]) + chan_inbias[:, cs]
+            grad = dot_nt(ups[at, :], w2[cs, :])
+            activ, slope = gelu_and_slope(inner)
+            act_s[at, :] = activ.astype(BF16)
+            gi = grad * slope
+            gi_s[at, :] = gi.astype(BF16)
+            total += jnp.sum(gi, axis=0, keepdims=True)
+        d_b1[:, cs] = total
+        g_out = dot(ups_t[...], act_s[...]).astype(BF16)
+        g_in = dot(sec_t[...], gi_s[...]).astype(BF16)
+        for n in range(1):
+            c = b * (1) + n
+            blk[c, 0] = g_in[:, n * FC : (n + 1) * FC]
+            blk[c, 1] = g_out[:, n * FC : (n + 1) * FC]
         gsec[...] += dot_nt(gi_s[...], w1[:, cs])
-        blk[c, 0] = dot(sec_t[...], gi_s[...]).astype(BF16)
-        blk[c, 1] = dot(ups_t[...], act_s[...]).astype(BF16)
 
     def image_backward(i):
         for q in peers:
@@ -368,12 +386,6 @@
         return_own(mo, patch_grad, ps_s, i).start()
 
     def pack_small():
-        for j in range(ds // 128):
-            cols = slice(j * 128, (j + 1) * 128)
-            blk[nc, 0, j * rows : (j + 1) * rows, :128] = d_tin[:, cols].astype(BF16)
-            blk[nc, 1, j * rows : (j + 1) * rows, :128] = d_tout[:, cols].astype(BF16)
-        blk[nc, 0, :, 128:] = jnp.zeros((width, 128), BF16)
-        blk[nc, 1, :, 128:] = jnp.zeros((width, 128), BF16)
         at = 0
         for v, n in (
             [(vecs[k : k + 1, :], width) for k in range(5)]
@@ -381,83 +393,117 @@
             + [(d_b1[...], dc)]
         ):
             for j in range(n // 128):
-                rows32[at : at + 1, :128] = v[:, j * 128 : (j + 1) * 128]
+                r = spare_row(at, part)
+                d_tin[r : r + 1, :128] = v[:, j * 128 : (j + 1) * 128]
                 at += 1
-        up = -(-at // 16) * 16
-        blk[nc, 0, :up, 128:] = rows32[:up, :128].astype(BF16)
-
-    def stage_device(k, c):
-        swap = lax.rem(c, 4) // 3
-        dev1 = (dev_y[0] + swap * (dp - dev_y[0]), me + swap * (xp - me))
-        dev4 = (dp + swap * (dev_y[0] - dp), xp + swap * (me - xp))
-        return (dev_sib, dev1, dev_za, dev_zb, dev4, dev_zb, dev_za, dev1, dev_sib)[k]
-
-    def stage(k, c):
-        swap = lax.rem(c, 4) // 3
-        b1 = yb + swap * (xb - yb)
-        half, quarter, eighth = width // 2, width // 4, width // 8
-        o1 = b1 * half
-        n1 = (1 - b1) * half
-        o2 = o1 + zab * quarter
-        n2 = o1 + (1 - zab) * quarter
-        o3 = o2 + zbb * eighth
-        n3 = o2 + (1 - zbb) * eighth
-        own = blk.at[c, core]
-
-        def piece(start, size):
-            return own.at[pl.ds(pl.multiple_of(start, 16), size), :]
-
-        kept = (own, piece(o1, half), piece(o2, quarter), piece(o3, eighth), piece(o3, eighth))
-        src = (
-            blk.at[c, 1 - core],
-            piece(n1, half),
-            piece(n2, quarter),
-            piece(n3, eighth),
-            piece(o3, eighth),
-            piece(o3, eighth),
-            piece(o2, quarter),
-            piece(o1, half),
-            own,
-        )[k]
-        land = (r0.at[lax.rem(c, 4)], r1.at[c], r2.at[c], r3.at[c], r4.at[c])
-        copy = pltpu.make_async_remote_copy(
-            src_ref=src,
-            dst_ref=land[k] if k < 5 else src,
-            send_sem=as_s.at[k, c],
-            recv_sem=as_r.at[k, c],
-            device_id=stage_device(k, c),
-            device_id_type=MESH,
-        )
-        return copy, (kept[k] if k < 5 else None), (land[k] if k < 5 else None)
+        for j in range(ds // 128):
+            cols = slice(j * 128, (j + 1) * 128)
+            blk[nc, 0, j * rows : (j + 1) * rows, :128] = d_tin[:, cols].astype(BF16)
+            blk[nc, 1, j * rows : (j + 1) * rows, :128] = d_tout[:, cols].astype(BF16)
+        blk[nc, :, :, 128:] = jnp.zeros((2, width, FC - 128), BF16)
+
+    def parts(k, c, lanes):
+        def region(m, start, size):
+            return blk.at[c, m, pl.ds(pl.multiple_of(start, 16), size), pl.ds(0, lanes)]
+
+        def transfer(slot, src, dst, dev):
+            return pltpu.make_async_remote_copy(
+                src_ref=src,
+                dst_ref=dst,
+                send_sem=as_s.at[slot, c],
+                recv_sem=as_r.at[slot, c],
+                device_id=dev,
+                device_id_type=MESH,
+            )
+
+        if k == 0:
+            land = r0.at[lax.rem(c, 4), :, pl.ds(0, lanes)]
+            copy = transfer(0, region(1 - core, 0, width), land, dev_sib)
+            return [(0, copy, region(core, 0, width), land, dev_sib)]
+        if k == 8:
+            own = region(core, 0, width)
+            return [(1, transfer(1, own, own, dev_sib), None, None, dev_sib)]
+        out = []
+        for n, (base, size, first, b1, final) in enumerate(
+            (
+                (0, SPLIT, dev_y, yb, dev_x),
+                (SPLIT, width - SPLIT, dev_x, xb, dev_y),
+            )
+        ):
+            half, quarter, eighth = size // 2, size // 4, size // 8
+            o1 = base + b1 * half
+            n1 = base + (1 - b1) * half
+            o2 = o1 + zab * quarter
+            n2 = o1 + (1 - zab) * quarter
+            o3 = o2 + zbb * eighth
+            n3 = o2 + (1 - zbb) * eighth
+            dev = (first, dev_za, dev_zb, final, dev_zb, dev_za, first)[k - 1]
+            slot = 2 * k + n
+            if k < 5:
+                start, count = ((n1, half), (n2, quarter), (n3, eighth), (o3, eighth))[k - 1]
+                keep = ((o1, half), (o2, quarter), (o3, eighth), (o3, eighth))[k - 1]
+                offset = (0, SPLIT // 2 // (1, 2, 4, 4)[k - 1])[n]
+                land = (r1, r2, r3, r4)[k - 1].at[c, pl.ds(offset, count), pl.ds(0, lanes)]
+                copy = transfer(slot, region(core, start, count), land, dev)
+                out.append((slot, copy, region(core, *keep), land, dev))
+            else:
+                mine = region(core, *((o3, eighth), (o2, quarter), (o1, half))[k - 5])
+                out.append((slot, transfer(slot, mine, mine, dev), None, None, dev))
+        return out
 
     def export(c):
         return pltpu.make_async_copy(blk.at[c], sums.at[c], osem.at[c])
 
+    enter = nc + EXTRA
+
+    def done(n):
+        rest = jnp.maximum(n - LEAD, 0) * (nc + ni - LEAD) // (enter + 1 - LEAD)
+        return jnp.minimum(n, LEAD) + rest
+
+    def proceed(k, c, lanes):
+        following = parts(k + 1, c, lanes) if k < 8 else []
+        done = parts(k, c, lanes)
+        for n, (slot, copy, kept, land, dev) in enumerate(done):
+            copy.wait()
+            if k < 4:
+                pl.semaphore_signal(free.at[slot, c], inc=1, device_id=dev, device_id_type=MESH)
+            if kept is not None:
+                kept[...] = (kept[...].astype(F32) + land[...].astype(F32)).astype(BF16)
+            if len(following) == len(done):
+                begin(k + 1, c, following[n])
+        if len(following) != len(done):
+            for part_ in following:
+                begin(k + 1, c, part_)
+        if k == 8:
+            export(c).start()
+
+    def begin(k, c, part_):
+        slot, copy = part_[:2]
+        if k >= 5:
+            back = 0 if k == 8 else 2 * (8 - k) + slot % 2
+            pl.semaphore_wait(free.at[back, c], 1)
+        copy.start()
+
+    def advance(k, u):
+        e = u - WAIT[k]
+
+        @pl.when(jnp.logical_and(e >= 0, e < nc))
+        def _():
+            proceed(k, e, FC)
+
+        @pl.when(e == enter)
+        def _():
+            proceed(k, nc, FC // 2)
+
     def step(u, carry):
         for k in reversed(range(9)):
-            c = u - WAIT[k]
-
-            @pl.when(jnp.logical_and(c >= 0, c <= nc))
-            def _(k=k, c=c):
-                copy, kept, land = stage(k, c)
-                copy.wait()
-                if k < 4:
-                    dev = stage_device(k, c)
-                    pl.semaphore_signal(free.at[k, c], inc=1, device_id=dev, device_id_type=MESH)
-                if kept is not None:
-                    kept[...] = (kept[...].astype(F32) + land[...].astype(F32)).astype(BF16)
-                if k < 8:
-                    if k >= 4:
-                        pl.semaphore_wait(free.at[7 - k, c], 1)
-                    stage(k + 1, c)[0].start()
-                else:
-                    export(c).start()
+            advance(k, u)
 
         @pl.when(u < ni)
         def _():
             send_mixed(u)
 
-        @pl.when(u <= nc)
+        @pl.when(u <= enter)
         def _():
             def quantum(w, carry):
                 @pl.when(w < nc)
@@ -470,23 +516,20 @@
 
                 return carry
 
-            lead = nc // 2
-
-            def done(n):
-                rest = jnp.maximum(n - lead, 0) * (nc + ni - lead) // (nc + 1 - lead)
-                return jnp.minimum(n, lead) + rest
-
             lax.fori_loop(done(u), done(u + 1), quantum, 0)
 
-            @pl.when(u == nc)
-            def _():
-                pack_small()
-
-            stage(0, u)[0].start()
+        @pl.when(u < nc)
+        def _():
+            begin(0, u, parts(0, u, FC)[0])
+
+        @pl.when(u == enter)
+        def _():
+            pack_small()
+            begin(0, nc, parts(0, nc, FC // 2)[0])
 
         return carry
 
-    lax.fori_loop(0, nc + 1 + WAIT[-1], step, 0)
+    lax.fori_loop(0, enter + 1 + WAIT[-1], step, 0)
 
     def finish(i):
         for q in peers:
@@ -545,7 +588,7 @@
         for copy in loads:
             copy.start()
 
-    @pl.when(pl.program_id(0) == 3)
+    @pl.when(pl.program_id(0) == pl.num_programs(0) // 2)
     def _():
         for load, store in zip(loads, stores):
             load.wait()
@@ -556,8 +599,9 @@
         for store in stores:
             store.wait()
 
-    chan_in[...] = block[0, 0].astype(F32)
-    chan_out[...] = block[0, 1].astype(F32).T
+    for n in range(WIDE):
+        chan_in[:, n * FC : (n + 1) * FC] = block[n, 0].astype(F32)
+        chan_out[n * FC : (n + 1) * FC, :] = block[n, 1].astype(F32).T
 
     @pl.when(pl.program_id(0) == 0)
     def _():
@@ -568,7 +612,7 @@
                     ref[s * part : (s + 1) * part, j * 128 : (j + 1) * 128] = v[
                         s * SLAB : s * SLAB + part
                     ]
-        v = small[0, 0, :rows, 128:].astype(F32)
+        v = small[0, 0, :rows, :128].astype(F32)
         at = 0
         for ref, n in (
             (gain_one, width),
@@ -580,7 +624,8 @@
             (tok_outbias, rows),
             (chan_inbias, dc),
         ):
-            flat = jnp.concatenate([v[at + j : at + j + 1] for j in range(n // 128)], axis=1)
+            picked = [spare_row(at + j, part) for j in range(n // 128)]
+            flat = jnp.concatenate([v[r : r + 1] for r in picked], axis=1)
             at += n // 128
             if ref is tok_outbias:
                 flat = jnp.concatenate(
@@ -673,8 +718,8 @@
             dma((nc + 1,)),
         ]
         + [dma((ni, 4))] * 8
-        + [dma((9, nc + 1))] * 2
-        + [pltpu.SemaphoreType.REGULAR((4, nc + 1))],
+        + [dma((16, nc + 1))] * 2
+        + [pltpu.SemaphoreType.REGULAR((8, nc + 1))],
         compiler_params=pltpu.CompilerParams(
             collective_id=0, has_side_effects=True, vmem_limit_bytes=63 << 20
         ),
@@ -705,7 +750,7 @@
     out = pl.pallas_call(
         functools.partial(spread_kernel, dims),
         name="spread",
-        grid=(nc,),
+        grid=(nc // WIDE,),
         out_shape=(
             jax.ShapeDtypeStruct((width, dc), F32),
             jax.ShapeDtypeStruct((dc, width), F32),
@@ -718,14 +763,14 @@
             jax.ShapeDtypeStruct(patches.shape, BF16),
         ),
         in_specs=[
-            pl.BlockSpec((1, 2, width, FC), lambda c: (c, 0, 0, 0)),
+            pl.BlockSpec((WIDE, 2, width, FC), lambda c: (c, 0, 0, 0)),
             pl.BlockSpec((1, 2, width, FC), lambda c: (nc, 0, 0, 0)),
             anywhere,
             anywhere,
         ],
         out_specs=(
-            pl.BlockSpec((width, FC), lambda c: (0, c)),
-            pl.BlockSpec((FC, width), lambda c: (c, 0)),
+            pl.BlockSpec((width, WIDE * FC), lambda c: (0, c)),
+            pl.BlockSpec((WIDE * FC, width), lambda c: (c, 0)),
             pl.BlockSpec((s_all, ds), lambda c: (0, 0)),
             pl.BlockSpec((s_all, ds), lambda c: (0, 0)),
         )

time: 221 us -> 204 us (0.923)
  Pallas kernels: 219 us -> 203 us
    pallas_call x1, Pallas kernels: 203 us -> 189 us  [shards(): pl.pallas_call(functools.partial(layer_kernel, dims), name='layer', out_s...]
    pallas_call x1, Pallas kernels: 16.7 us -> 14 us  [shards(): pl.pallas_call(functools.partial(spread_kernel, dims), name='spread', gri...]
where the time goes in v3:
time: 204 us
  Pallas kernels  203 us (100%)
    pallas_call x1, Pallas kernels, shards(): pl.pallas_call(functools.partial(layer_kernel, dims), name='layer', out_s...  189 us
    pallas_call x1, Pallas kernels, shards(): pl.pallas_call(functools.partial(spread_kernel, dims), name='spread', gri...  14 us

profile of v3, /device:TPU:0, one launch (start us, length us, event | category | flops | bytes accessed | tf_op | source)
XLA Modules:
  0.0 204.0 jit_solution(7942852370647783562)
XLA Ops:
  1.3 188.7 %layer.1 = (bf16[28,49,768]{2,1,0:T(8,128)(2,1)}, bf16[28,49,768]{2,1,0:T(8,128)(2,1)}, bf16[13,2,768,256]{3,2,1,0:T(8,128)(2,1)}) custom-call(bf16[28,49,768]{2,1,0:T(8,128)(2,1)} %patches.1, bf16[28,49,768]{2,1,0:T(8,128)(2,1)} %out_grad.1, s32[1]{0:T(128)S(6)} %copy.29.valid, bf16[196,384]{1,0:T(8,128)(2,1)} %tok_in.1, bf16[196,384]{1,0:T(8,128)(2,1)} %bitcast.4, ...), custom_call_target="tpu_custom_call" | custom-call | flops 59190018048 | bytes 41943040 | tf_op jit(solution)/shard_map/layer/pallas_call | solution.py:666
  190.0 14.0 %spread.1 = (f32[768,3072]{1,0:T(8,128)}, f32[3072,768]{1,0:T(8,128)}, f32[196,384]{1,0:T(8,128)}, f32[196,384]{1,0:T(8,128)}, f32[768]{0:T(1024)}, /*index=5*/f...) custom-call(bf16[13,2,768,256]{3,2,1,0:T(8,128)(2,1)} %get-tuple-ele, ...), custom_call_target="tpu_custom_call" | custom-call | tf_op jit(solution)/shard_map/spread/pallas_call | solution.py:750

commit v4 on v3

--- a/solution.py
+++ b/solution.py
@@ -410,7 +410,7 @@
             return pltpu.make_async_remote_copy(
                 src_ref=src,
                 dst_ref=dst,
-                send_sem=as_s.at[slot, c],
+                send_sem=as_s.at[slot, lax.rem(c, 4)],
                 recv_sem=as_r.at[slot, c],
                 device_id=dev,
                 device_id_type=MESH,
@@ -718,7 +718,7 @@
             dma((nc + 1,)),
         ]
         + [dma((ni, 4))] * 8
-        + [dma((16, nc + 1))] * 2
+        + [dma((16, 4)), dma((16, nc + 1))]
         + [pltpu.SemaphoreType.REGULAR((8, nc + 1))],
         compiler_params=pltpu.CompilerParams(
             collective_id=0, has_side_effects=True, vmem_limit_bytes=63 << 20

time: 204 us -> 203 us (level)
  no operation moved by 1% of the time
where the time goes in v4:
time: 203 us
  Pallas kernels  201 us (99%)
    pallas_call x1, Pallas kernels, shards(): pl.pallas_call(functools.partial(layer_kernel, dims), name='layer', out_s...  187 us
    pallas_call x1, Pallas kernels, shards(): pl.pallas_call(functools.partial(spread_kernel, dims), name='spread', gri...  14 us

profile of v4, /device:TPU:0, one launch (start us, length us, event | category | flops | bytes accessed | tf_op | source)
XLA Modules:
  0.0 202.7 jit_solution(13692463142841806659)
XLA Ops:
  1.3 187.4 %layer.1 = (bf16[28,49,768]{2,1,0:T(8,128)(2,1)}, bf16[28,49,768]{2,1,0:T(8,128)(2,1)}, bf16[13,2,768,256]{3,2,1,0:T(8,128)(2,1)}) custom-call(bf16[28,49,768]{2,1,0:T(8,128)(2,1)} %patches.1, bf16[28,49,768]{2,1,0:T(8,128)(2,1)} %out_grad.1, s32[1]{0:T(128)S(6)} %copy.29.valid, bf16[196,384]{1,0:T(8,128)(2,1)} %tok_in.1, bf16[196,384]{1,0:T(8,128)(2,1)} %bitcast.4, ...), custom_call_target="tpu_custom_call" | custom-call | flops 59190018048 | bytes 41943040 | tf_op jit(solution)/shard_map/layer/pallas_call | solution.py:666
  188.7 14.0 %spread.1 = (f32[768,3072]{1,0:T(8,128)}, f32[3072,768]{1,0:T(8,128)}, f32[196,384]{1,0:T(8,128)}, f32[196,384]{1,0:T(8,128)}, f32[768]{0:T(1024)}, /*index=5*/f...) custom-call(bf16[13,2,768,256]{3,2,1,0:T(8,128)(2,1)} %get-tuple-ele, ...), custom_call_target="tpu_custom_call" | custom-call | tf_op jit(solution)/shard_map/spread/pallas_call | solution.py:750
